TPU v7x, 32 devices: a whole 2x2x4 slice. The times are simulated.
32 devices in a mesh: group: 8 (over z, core), tensor: 4 (over y, x).
Axes of the slice: x: 2, y: 2, z: 4, core: 2. Of those that a mesh axis runs over, the one named last changes fastest.
Arguments:
- queries: bfloat16 [96, 4, 8192], P('group', None, 'tensor'), may hold values from -603 to 603
- new_entries: bfloat16 [96, 4, 2048], P('group'), may hold values from -6 to 6
- resident_cache: bfloat16 [32, 512, 2048], P('group', 'tensor'), may hold values from -6 to 6
- prefill_cache: bfloat16 [64, 512, 2048], P('group', 'tensor'), may hold values from -6 to 6
- resident_kept: int32 [32], replicated, may hold values from 256 to 512, as said below
- kept_tokens: int32 [64], replicated, may hold values from 1 to 512, as said below
- prefill_slot: int32 [64], replicated, may hold values from 0 to 63, as said below
- decode_slot: int32 [64], replicated, may hold values from 4 to 95, as said below
Outputs:
- attended: bfloat16 [96, 4, 8192], P('group', None, 'tensor')
Inputs may be any that keep to these rules, and one draw needn't show every extreme that they name: `kept_tokens`: some request keeps exactly 512 positions. `prefill_slot`: A permutation of the 64 prefill slots; slot s lies in prefill group s // 8. `decode_slot`: every slot g * 12 + l with l >= 4 is named by exactly one request; from one prefill group to one decode group go at most 1 request, and exactly 1 for some pairs. `resident_kept`: some resident request keeps exactly 512 positions.
All inputs are finite; a program needn't handle non-finite values.
Results may differ from a plain program's by a relative error of at most 0.0044.
Values may be sent and summed in bfloat16 or wider, within the bound.
A program may use at most 128 MiB of HBM per device.

v0:
```python
import functools
import math

import jax
import jax.numpy as jnp
from jax import lax
from jax.experimental import pallas as pl
from jax.experimental.pallas import tpu as pltpu
from jax.sharding import PartitionSpec as P

H = 64
KVH = 8
HD = 128
STEPS = 4
MIG_DEV = 8
RES_DEV = 4
PER_GROUP = RES_DEV + MIG_DEV
BATCH = 4

NEG_FLOOR = -1e30
SCALE = 1.0 / math.sqrt(HD)
MESH = pl.DeviceIdType.MESH
F32 = jnp.float32
BF16 = jnp.bfloat16
NT = (((1,), (1,)), ((), ()))
TN = (((0,), (0,)), ((), ()))


def fill_table(G, g, kept_v, home_v, dest_v, tab_v):
    shape = (2 * G, dest_v.shape[1])
    n = lax.broadcasted_iota(jnp.int32, shape, 0)
    dest = jnp.broadcast_to(dest_v[...], shape)
    home = jnp.broadcast_to(home_v[...], shape)
    kept = jnp.broadcast_to(kept_v[...], shape)
    dest_group, home_group = lax.div(dest, PER_GROUP), lax.div(home, MIG_DEV)
    arriving = (dest_group == g) & (home_group == n)
    leaving = (home_group == g) & (dest_group == n - G)
    picked = jnp.where(arriving, dest - dest_group * PER_GROUP, 0)
    held = home - home_group * MIG_DEV + MIG_DEV * kept
    picked = picked + jnp.where(leaving, held, 0)
    total = jnp.sum(picked, axis=1, keepdims=True)
    tab_v[...] = jnp.broadcast_to(total, tab_v.shape)


def kernel(
    G,
    T,
    kept_v,
    home_v,
    dest_v,
    kept,
    q_hbm,
    new_hbm,
    res_hbm,
    pre_hbm,
    out,
    tab_v,
    tab_s,
    q_in,
    new_in,
    res,
    pre,
    qall,
    zq,
    stage,
    obuf,
    rbuf,
    sbuf,
    rstat,
    statbuf,
    facbuf,
    zo,
    zro,
    zs,
    zrs,
    newk,
    nstat,
    nadd,
    fin,
    cache_sem,
    zq_s,
    zq_r,
    rq_s,
    rq_r,
    f_s,
    f_r,
    o_s,
    o_r,
    st_s,
    st_r,
    zo_s,
    zo_r,
    zs_s,
    zs_r,
):
    KVL = max(1, KVH // T)
    HB = H // T
    HU = HB // KVL
    R = STEPS * HU
    LW = BATCH * R
    SW = 2 * KVL
    NB = 1 + G // BATCH
    pos = res.shape[1]
    half = KVH * HD
    g = lax.axis_index("group")
    t = lax.axis_index("tensor")
    offset = t * pos

    def peer_t(k):
        return lax.rem(t + k, T)

    def peer_g(k):
        return lax.rem(g + k, G)

    def from_g(k):
        return lax.rem(g - k + G, G)

    def over_t(src, dst, ssem, rsem, dev):
        return pltpu.make_async_remote_copy(
            src_ref=src, dst_ref=dst, send_sem=ssem, recv_sem=rsem,
            device_id=(g, dev), device_id_type=MESH,
        )

    def over_g(src, dst, ssem, rsem, dev):
        return pltpu.make_async_remote_copy(
            src_ref=src, dst_ref=dst, send_sem=ssem, recv_sem=rsem,
            device_id=(dev, t), device_id_type=MESH,
        )

    def c_zq(k):
        return over_g(zq.at[k], qall.at[t, RES_DEV + k], zq_s.at[0], zq_r.at[k], peer_g(k))

    def c_rq(k):
        p = peer_t(k)
        own = qall.at[t, pl.ds(0, RES_DEV)]
        return over_t(own, own, rq_s.at[0], rq_r.at[0], p)

    def c_fwd(k, n):
        own = qall.at[t, RES_DEV + k]
        return over_t(own, own, f_s.at[n], f_r.at[k], peer_t(n))

    def c_o(b, j, n):
        p = peer_t(n)
        rows = pl.ds(pl.multiple_of(j * R, R), R)
        return over_t(
            obuf.at[b, p, :, rows], rbuf.at[b, n, :, rows], o_s.at[b], o_r.at[b], p
        )

    def c_st(b, n):
        p = peer_t(n)
        return over_t(sbuf.at[b, p], rstat.at[b, n], st_s.at[b], st_r.at[b], p)

    def c_zo(k):
        return over_g(zo.at[k], zro.at[k], zo_s.at[0], zo_r.at[k // BATCH], from_g(k))

    def c_zs(k):
        return over_g(zs.at[k // BATCH], zrs.at[k], zs_s.at[0], zs_r.at[k // BATCH], from_g(k))

    barrier = pltpu.get_barrier_semaphore()
    for k in range(G - 1, 0, -1):
        pl.semaphore_signal(barrier, inc=1, device_id=(peer_g(k), t), device_id_type=MESH)
    for k in range(1, T):
        pl.semaphore_signal(barrier, inc=1, device_id=(g, peer_t(k)), device_id_type=MESH)
    load_q = pltpu.make_async_copy(q_hbm, q_in, cache_sem.at[2])
    load_new = pltpu.make_async_copy(new_hbm, new_in, cache_sem.at[3])
    load_res = pltpu.make_async_copy(res_hbm, res, cache_sem.at[0])
    load_pre = pltpu.make_async_copy(pre_hbm, pre, cache_sem.at[1])
    load_q.start()
    load_new.start()
    load_pre.start()
    load_res.start()
    fill_table(G, g, kept_v, home_v, dest_v, tab_v)
    load_tab = pltpu.make_async_copy(tab_v, tab_s, cache_sem.at[4])
    load_tab.start()
    load_tab.wait()
    load_q.wait()

    def arranged(row, slot):
        for h in range(HB):
            piece = q_in[row, :, h * HD : (h + 1) * HD]
            stage[slot, h * STEPS : (h + 1) * STEPS, :] = piece.astype(F32)
        return stage[slot].astype(BF16)

    for k in range(G):
        block = arranged(tab_s[peer_g(k), 0], k)
        zq[k] = block
        if k == 0:
            qall[t, RES_DEV] = block
    for j in range(RES_DEV):
        qall[t, j] = arranged(j, G + j)

    pl.semaphore_wait(barrier, G - 1 + T - 1)
    for k in range(1, G):
        c_zq(k).start()
    for n in range(1, T):
        c_rq(n).start()
    for n in range(1, T):
        c_fwd(0, n).start()

    load_new.wait()
    kv_col = pl.multiple_of((t * KVL * KVH) // (T * KVL) * HD, HD)
    for b in range(NB):
        for j in range(BATCH):
            row = j if b == 0 else tab_s[peer_g((b - 1) * BATCH + j), 0]
            lo = j * STEPS
            newk[b, 0, lo : lo + STEPS, :] = new_in[row, :, pl.ds(kv_col, KVL * HD)].astype(F32)
            newk[b, 1, lo : lo + STEPS, :] = new_in[
                row, :, pl.ds(pl.multiple_of(half + kv_col, HD), KVL * HD)
            ].astype(F32)

    def queries_of(b):
        return [
            jnp.concatenate(
                [
                    (qall[t, j] if b == 0 else zq[(b - 1) * BATCH + j])[i * R : (i + 1) * R]
                    for j in range(BATCH)
                ],
                axis=0,
            )
            for i in range(KVL)
        ]

    r16 = lax.broadcasted_iota(jnp.int32, (BATCH * STEPS, LW), 0)
    lanes16 = lax.broadcasted_iota(jnp.int32, (BATCH * STEPS, LW), 1)
    causal = (r16 // STEPS == lanes16 // R) & (r16 % STEPS <= lanes16 % STEPS)
    for b in range(NB):
        asked_b = queries_of(b)
        for i in range(KVL):
            keys = newk[b, 0, :, i * HD : (i + 1) * HD].astype(BF16)
            values = newk[b, 1, :, i * HD : (i + 1) * HD].astype(BF16)
            scores = lax.dot_general(keys, asked_b[i], NT, preferred_element_type=F32) * SCALE
            scores = jnp.where(causal, scores, NEG_FLOOR)
            top = jnp.max(scores, axis=0, keepdims=True)
            weights = jnp.where(causal, jnp.exp(scores - top), 0.0)
            nstat[b, i : i + 1, :] = top
            nstat[b, KVL + i : KVL + i + 1, :] = jnp.sum(weights, axis=0, keepdims=True)
            nadd[b, i] = lax.dot_general(
                weights.astype(BF16), values, TN, preferred_element_type=F32
            )

    for k in range(1, G):
        c_zq(k).wait_recv()
        for n in range(1, T):
            c_fwd(k, n).start()

    def attend_slot(cache, row, length, slot, b, j):
        lane = lax.broadcasted_iota(jnp.int32, (R, 128), 1)
        usable = offset + lax.broadcasted_iota(jnp.int32, (R, pos), 1) < length
        stat = jnp.zeros((R, 128), F32)
        rows = pl.ds(pl.multiple_of(j * R, R), R)
        W = 2 if KVL % 2 == 0 else 1
        units = [(tt, i) for tt in range(T) for i in range(0, KVL, W)]
        all_scores = []
        for tt, i in units:
            kv = (tt * KVL + i) * KVH // (T * KVL)
            asked = qall[tt, slot, i * R : (i + W) * R, :]
            keys = jnp.concatenate(
                [cache[row, :, (kv + w) * HD : (kv + w + 1) * HD] for w in range(W)], axis=0
            )
            scores = lax.dot_general(asked, keys, NT, preferred_element_type=F32)
            all_scores.append(
                [scores[w * R : (w + 1) * R, w * pos : (w + 1) * pos] * SCALE for w in range(W)]
            )
        all_weights = []
        for (tt, i), scores in zip(units, all_scores):
            rounded = []
            for w in range(W):
                masked = jnp.where(usable, scores[w], NEG_FLOOR)
                highest = jnp.max(masked, axis=1, keepdims=True)
                weights = jnp.where(usable, jnp.exp(masked - highest), 0.0)
                total = jnp.sum(weights, axis=1, keepdims=True)
                rounded.append(weights.astype(BF16))
                stat = jnp.where(lane == tt * SW + i + w, highest, stat)
                stat = jnp.where(lane == tt * SW + KVL + i + w, total, stat)
            all_weights.append(jnp.concatenate(rounded, axis=0))
        for (tt, i), weights in zip(units, all_weights):
            kv = (tt * KVL + i) * KVH // (T * KVL)
            values = cache[row, :, half + kv * HD : half + (kv + W) * HD]
            blended = jnp.dot(weights, values, preferred_element_type=F32)
            for w in range(W):
                obuf[b, tt, i + w, rows, :] = blended[
                    w * R : (w + 1) * R, w * HD : (w + 1) * HD
                ].astype(BF16)
        statbuf[rows, :] = stat
        for n in range(1, T):
            c_o(b, j, n).start()

    def send_batch(b):
        turned = statbuf[...].T
        for tt in range(T):
            sbuf[b, tt] = turned[tt * SW : tt * SW + 8, :]
        for n in range(1, T):
            c_st(b, n).start()
        rbuf[b, 0] = obuf[b, t]
        rstat[b, 0] = sbuf[b, t]

    rest = pl.ds(1, T - 1)
    load_pre.wait()

    @pl.loop(1, NB)
    def _(b):
        @pl.loop(0, BATCH)
        def _(j):
            k = (b - 1) * BATCH + j
            spread = qall.at[rest, RES_DEV + k]
            over_t(spread, spread, f_s.at[0], f_r.at[k], t).wait_recv()
            source = from_g(k)
            held = tab_s[G + source, 0]
            attend_slot(pre, held % MIG_DEV, held // MIG_DEV, RES_DEV + k, b, j)

        send_batch(b)

    load_res.wait()
    q_rest = qall.at[rest, pl.ds(0, RES_DEV)]
    over_t(q_rest, q_rest, rq_s.at[0], rq_r.at[0], t).wait_recv()

    @pl.loop(0, RES_DEV)
    def _(j):
        attend_slot(res, j, kept[g * RES_DEV + j], j, 0, j)

    send_batch(0)
    def merged(b):
        over_t(rstat.at[b, rest], rstat.at[b, rest], st_s.at[b], st_r.at[b], t).wait_recv()
        over_t(rbuf.at[b, rest], rbuf.at[b, rest], o_s.at[b], o_r.at[b], t).wait_recv()
        tops = [rstat[b, n][:KVL] for n in range(T)]
        highest = functools.reduce(jnp.maximum, tops)
        total = jnp.zeros((KVL, LW), F32)
        for n in range(T):
            factor = jnp.exp(tops[n] - highest)
            total = total + factor * rstat[b, n][KVL:SW]
            facbuf[n * KVL : (n + 1) * KVL, :] = factor
        columns = facbuf[...].T
        blended = []
        for i in range(KVL):
            sum_i = jnp.zeros((LW, HD), F32)
            for n in range(T):
                c = n * KVL + i
                sum_i = sum_i + rbuf[b, n, i].astype(F32) * columns[:, c : c + 1]
            blended.append(sum_i)
        return highest, total, blended

    def finish(b, highest, total, blended):
        new_top, new_total = nstat[b, 0:KVL], nstat[b, KVL:SW]
        top = jnp.maximum(highest, new_top)
        old_part, new_part = jnp.exp(highest - top), jnp.exp(new_top - top)
        inverse = 1.0 / (total * old_part + new_total * new_part)
        facbuf[0:KVL, :] = old_part * inverse
        facbuf[KVL:SW, :] = new_part * inverse
        columns = facbuf[...].T
        for i in range(KVL):
            done = blended[i] * columns[:, i : i + 1]
            done = done + nadd[b, i] * columns[:, KVL + i : KVL + i + 1]
            for j in range(BATCH):
                fin[b * BATCH + j, i * R : (i + 1) * R, :] = done[j * R : (j + 1) * R]

    def put(slot, row):
        for h in range(HB):
            piece = fin[slot, h * STEPS : (h + 1) * STEPS, :]
            out[row, :, h * HD : (h + 1) * HD] = piece.astype(BF16)

    for b in range(1, NB):
        highest, total, blended = merged(b)
        packed = jnp.concatenate([highest, total], axis=0)
        zs[b - 1, 0:SW, :] = packed
        for j in range(BATCH):
            k = (b - 1) * BATCH + j
            for i in range(KVL):
                zo[k, i] = blended[i][j * R : (j + 1) * R].astype(BF16)
            if k:
                c_zs(k).start()
                c_zo(k).start()
            else:
                zrs[0] = zs[0]
                zro[0] = zo[0]

    finish(0, *merged(0))
    for j in range(RES_DEV):
        put(j, j)

    for b in range(1, NB):
        lanes = lax.broadcasted_iota(jnp.int32, (8, LW), 1)
        stats = jnp.zeros((8, LW), F32)
        first = (b - 1) * BATCH
        came = pl.ds(max(first, 1), first + BATCH - max(first, 1))
        over_g(zrs.at[came], zrs.at[came], zs_s.at[0], zs_r.at[b - 1], g).wait_recv()
        over_g(zro.at[came], zro.at[came], zo_s.at[0], zo_r.at[b - 1], g).wait_recv()
        for j in range(BATCH):
            k = (b - 1) * BATCH + j
            stats = jnp.where(lanes // R == j, zrs[k], stats)
        blended = [
            jnp.concatenate(
                [zro[(b - 1) * BATCH + j, i].astype(F32) for j in range(BATCH)], axis=0
            )
            for i in range(KVL)
        ]
        finish(b, stats[:KVL], stats[KVL:SW], blended)
    for l in range(MIG_DEV):
        k_of = 0
        for k in range(1, G):
            k_of = jnp.where(tab_s[peer_g(k), 0] == RES_DEV + l, k, k_of)
        put(RES_DEV + k_of, RES_DEV + l)

    others = pl.ds(1, G - 1)
    over_g(zq.at[others], zq.at[others], zq_s.at[0], zq_r.at[0], g).wait_send()
    over_g(zrs.at[others], zrs.at[others], zs_s.at[0], zs_r.at[0], g).wait_send()
    over_g(zo.at[others], zo.at[others], zo_s.at[0], zo_r.at[0], g).wait_send()
    over_t(q_rest, q_rest, rq_s.at[0], rq_r.at[0], t).wait_send()
    passed = qall.at[0, pl.ds(RES_DEV, G)]
    for n in range(1, T):
        over_t(passed, passed, f_s.at[n], f_r.at[0], t).wait_send()
    for b in range(NB):
        over_t(rstat.at[b, rest], rstat.at[b, rest], st_s.at[b], st_r.at[b], t).wait_send()
        over_t(rbuf.at[b, rest], rbuf.at[b, rest], o_s.at[b], o_r.at[b], t).wait_send()


def body(
    queries,
    new_entries,
    resident_cache,
    prefill_cache,
    resident_kept,
    kept_tokens,
    prefill_slot,
    decode_slot,
):
    G = lax.axis_size("group")
    T = lax.axis_size("tensor")
    KVL = max(1, KVH // T)
    HB = H // T
    RB = STEPS * HB
    R = RB // KVL
    LW = BATCH * R
    NB = 1 + G // BATCH
    dma = pltpu.SemaphoreType.DMA
    vmem = pl.BlockSpec(memory_space=pltpu.VMEM)
    smem = pl.BlockSpec(memory_space=pltpu.SMEM)
    hbm = pl.BlockSpec(memory_space=pl.ANY)
    return pl.pallas_call(
        functools.partial(kernel, G, T),
        out_shape=pltpu.VMEM(queries.shape, BF16),
        in_specs=[vmem, vmem, vmem, smem, hbm, hbm, hbm, hbm],
        out_specs=vmem,
        scratch_shapes=[
            pltpu.VMEM((2 * G, 128), jnp.int32),
            pltpu.SMEM((2 * G, 128), jnp.int32),
            pltpu.VMEM(queries.shape, BF16),
            pltpu.VMEM(new_entries.shape, BF16),
            pltpu.VMEM(resident_cache.shape, BF16),
            pltpu.VMEM(prefill_cache.shape, BF16),
            pltpu.VMEM((T, RES_DEV + G, RB, HD), BF16),
            pltpu.VMEM((G, RB, HD), BF16),
            pltpu.VMEM((G + RES_DEV, RB, HD), F32),
            pltpu.VMEM((NB, T, KVL, LW, HD), BF16),
            pltpu.VMEM((NB, T, KVL, LW, HD), BF16),
            pltpu.VMEM((NB, T, 8, LW), F32),
            pltpu.VMEM((NB, T, 8, LW), F32),
            pltpu.VMEM((LW, 128), F32),
            pltpu.VMEM((128, LW), F32),
            pltpu.VMEM((G, KVL, R, HD), BF16),
            pltpu.VMEM((G, KVL, R, HD), BF16),
            pltpu.VMEM((NB - 1, 8, LW), F32),
            pltpu.VMEM((G, 8, LW), F32),
            pltpu.VMEM((NB, 2, BATCH * STEPS, KVL * HD), F32),
            pltpu.VMEM((NB, 8, LW), F32),
            pltpu.VMEM((NB, KVL, LW, HD), F32),
            pltpu.VMEM((NB * BATCH, RB, HD), F32),
            dma((5,)),
            dma((1,)),
            dma((G,)),
            dma((1,)),
            dma((1,)),
            dma((T,)),
            dma((G,)),
            dma((NB,)),
            dma((NB,)),
            dma((NB,)),
            dma((NB,)),
            dma((1,)),
            dma((NB - 1,)),
            dma((1,)),
            dma((NB - 1,)),
        ],
        compiler_params=pltpu.CompilerParams(collective_id=0, has_side_effects=True),
    )(
        kept_tokens[None],
        prefill_slot[None],
        decode_slot[None],
        resident_kept,
        queries, new_entries, resident_cache, prefill_cache)


def solution(mesh):
    in_specs = (
        P("group", None, "tensor"),
        P("group", None, None),
        P("group", "tensor", None),
        P("group", "tensor", None),
        P(),
        P(),
        P(),
        P(),
    )
    out_specs = P("group", None, "tensor")
    return jax.shard_map(body, mesh=mesh, in_specs=in_specs, out_specs=out_specs, check_vma=False)
```

profile of v0, /device:TPU:0, one launch (start us, length us, event | category | flops | bytes accessed | tf_op | source)
XLA Modules:
  0.0 29.3 jit_solution(158352288912587101)
XLA Ops:
  0.0 28.6 %shard_map.82 = bf16[12,4,2048]{2,1,0:T(4,128)(2,1)S(1)} custom-call(s32[1,64]{1,0:T(1,128)} %bitcast.3, s32[1,64]{1,0:T(1,128)} %bitcast.4, s32[1,64]{1,0:T(1,128)} %bitcast.5, s32[32]{0:T(128)} %kept.1, bf16[12,4,2048]{2,1,0:T(4,128)(2,1)} %q_hbm.1, bf16[12,4,2048]{2,1,0:T(4,128)(2,1)} %new_hbm.1, bf16[4,128,2048]{2,1,0:T(8,128)(2,1)} %res_hbm.1, ...), custom_call_target="tpu_custom_call" | custom-call | tf_op jit(solution)/shard_map/pallas_call | solution.py:438
  28.6 0.7 %copy.10 = bf16[12,4,2048]{2,1,0:T(4,128)(2,1)} copy(bf16[12,4,2048]{2,1,0:T(4,128)(2,1)S(1)} %shard_map.82) | data formatting | bytes 393216
where the time goes:
time: 29.4 us; the launch traced here: 29.3 us
  Pallas kernels  28.6 us (97%)
  local copies, waits for them, and re-layouts  0.68 us (2%)
    pallas_call x1, Pallas kernels, body(): pl.pallas_call(functools.partial(kernel, G, T), out_shape=pltpu.VMEM(quer...  28.6 us
    unnamed x1, local copies, waits for them, and re-layouts  0.68 us

commit v1 on v0

--- a/solution.py
+++ b/solution.py
@@ -26,15 +26,29 @@
 TN = (((0,), (0,)), ((), ()))
 
 
-def fill_table(G, g, kept_v, home_v, dest_v, tab_v):
+def flipped(v, mask):
+    out, bit = v, 1
+    while bit <= mask:
+        if mask & bit:
+            out = out + bit * (1 - 2 * lax.rem(lax.div(v, bit), 2))
+        bit *= 2
+    return out
+
+
+def fill_table(peers, sources, g, kept_v, home_v, dest_v, tab_v):
+    G = len(peers)
     shape = (2 * G, dest_v.shape[1])
     n = lax.broadcasted_iota(jnp.int32, shape, 0)
     dest = jnp.broadcast_to(dest_v[...], shape)
     home = jnp.broadcast_to(home_v[...], shape)
     kept = jnp.broadcast_to(kept_v[...], shape)
     dest_group, home_group = lax.div(dest, PER_GROUP), lax.div(home, MIG_DEV)
-    arriving = (dest_group == g) & (home_group == n)
-    leaving = (home_group == g) & (dest_group == n - G)
+    other = jnp.zeros(shape, jnp.int32)
+    for k in range(G):
+        other = jnp.where(n == k, peers[k], other)
+        other = jnp.where(n == G + k, sources[k], other)
+    arriving = (n < G) & (dest_group == g) & (home_group == other)
+    leaving = (n >= G) & (home_group == g) & (dest_group == other)
     picked = jnp.where(arriving, dest - dest_group * PER_GROUP, 0)
     held = home - home_group * MIG_DEV + MIG_DEV * kept
     picked = picked + jnp.where(leaving, held, 0)
@@ -45,15 +59,19 @@
 def kernel(
     G,
     T,
-    kept_v,
-    home_v,
-    dest_v,
-    kept,
+    kept_hbm,
+    home_hbm,
+    dest_hbm,
+    stay_hbm,
     q_hbm,
     new_hbm,
     res_hbm,
     pre_hbm,
     out,
+    kept_v,
+    home_v,
+    dest_v,
+    kept,
     tab_v,
     tab_s,
     q_in,
@@ -78,12 +96,14 @@
     nadd,
     fin,
     cache_sem,
+    tab_sem,
+    above,
+    across,
     zq_s,
     zq_r,
-    rq_s,
-    rq_r,
-    f_s,
-    f_r,
+    q_s,
+    q_r1,
+    q_r2,
     o_s,
     o_r,
     st_s,
@@ -109,11 +129,20 @@
     def peer_t(k):
         return lax.rem(t + k, T)
 
+    paired = G & (G - 1) == 0
+    relay = T == 4
+    row_dev = t + 1 - 2 * lax.rem(t, 2)
+    col_dev = t + 2 - 4 * lax.div(t, 2)
+    greeted = (row_dev, col_dev, T - 1 - t) if relay else [lax.rem(t + n, T) for n in range(1, T)]
+
+    ways = list(dict.fromkeys((2, 3, G - 2, G - 1, *range(4, G), 1, 0)))
+    mine, beside = G - 1, G - 2
+
     def peer_g(k):
-        return lax.rem(g + k, G)
+        return flipped(g, ways[k]) if paired else lax.rem(g + ways[k], G)
 
     def from_g(k):
-        return lax.rem(g - k + G, G)
+        return peer_g(k) if paired else lax.rem(g - ways[k] + G, G)
 
     def over_t(src, dst, ssem, rsem, dev):
         return pltpu.make_async_remote_copy(
@@ -130,14 +159,30 @@
     def c_zq(k):
         return over_g(zq.at[k], qall.at[t, RES_DEV + k], zq_s.at[0], zq_r.at[k], peer_g(k))
 
-    def c_rq(k):
-        p = peer_t(k)
-        own = qall.at[t, pl.ds(0, RES_DEV)]
-        return over_t(own, own, rq_s.at[0], rq_r.at[0], p)
-
-    def c_fwd(k, n):
-        own = qall.at[t, RES_DEV + k]
-        return over_t(own, own, f_s.at[n], f_r.at[k], peer_t(n))
+    def relayed(s):
+        return relay and (s < RES_DEV or s - RES_DEV in (mine, beside))
+
+    def send_own(s):
+        own = qall.at[t, s]
+        if not relayed(s):
+            for dev in greeted:
+                over_t(own, own, q_s.at[0], q_r2.at[s], dev).start()
+            return
+        rows, cols = (q_r1, q_r2) if s % 2 == 0 else (q_r2, q_r1)
+        over_t(own, own, q_s.at[0], rows.at[s], row_dev).start()
+        over_t(own, own, q_s.at[0], cols.at[s], col_dev).start()
+
+    def pass_on(s):
+        if not relayed(s):
+            return
+        near, far = (row_dev, col_dev) if s % 2 == 0 else (col_dev, row_dev)
+        one = qall.at[near, s]
+        over_t(one, one, q_s.at[0], q_r1.at[s], far).wait_recv()
+        over_t(one, one, q_s.at[0], q_r2.at[s], far).start()
+
+    def whole(s, came):
+        rest = qall.at[pl.ds(0, came), s]
+        over_t(rest, rest, q_s.at[0], q_r2.at[s], t).wait_recv()
 
     def c_o(b, j, n):
         p = peer_t(n)
@@ -157,51 +202,96 @@
         return over_g(zs.at[k // BATCH], zrs.at[k], zs_s.at[0], zs_r.at[k // BATCH], from_g(k))
 
     barrier = pltpu.get_barrier_semaphore()
-    for k in range(G - 1, 0, -1):
+    moving = [k for k in range(G) if k != mine]
+
+    def when_above(k, act):
+        @pl.when(peer_g(k) > g)
+        def _():
+            act()
+
+    def when_below(k, act):
+        @pl.when(peer_g(k) < g)
+        def _():
+            act()
+
+    def greet(k):
         pl.semaphore_signal(barrier, inc=1, device_id=(peer_g(k), t), device_id_type=MESH)
-    for k in range(1, T):
-        pl.semaphore_signal(barrier, inc=1, device_id=(g, peer_t(k)), device_id_type=MESH)
+
+    def answer(k):
+        back = k if paired else ways.index((G - ways[k]) % G)
+        pl.semaphore_signal(
+            above.at[back], inc=1, device_id=(peer_g(k), t), device_id_type=MESH
+        )
+
+    def send_up(k):
+        pl.semaphore_wait(above.at[k], 1)
+        c_zq(k).start()
+
+    def late(k):
+        when_above(k, functools.partial(send_up, k))
+
+    def meet():
+        pl.semaphore_wait(barrier, g + (2 if relay else T - 1))
+        for k in moving:
+            when_below(k, functools.partial(answer, k))
+        if relay:
+            pl.semaphore_signal(
+                across.at[0], inc=1, device_id=(g, row_dev), device_id_type=MESH
+            )
+
+    for k in moving:
+        when_above(k, functools.partial(greet, k))
+    for dev in greeted[:2] if relay else greeted:
+        pl.semaphore_signal(barrier, inc=1, device_id=(g, dev), device_id_type=MESH)
     load_q = pltpu.make_async_copy(q_hbm, q_in, cache_sem.at[2])
     load_new = pltpu.make_async_copy(new_hbm, new_in, cache_sem.at[3])
     load_res = pltpu.make_async_copy(res_hbm, res, cache_sem.at[0])
     load_pre = pltpu.make_async_copy(pre_hbm, pre, cache_sem.at[1])
+    tables = [
+        pltpu.make_async_copy(src, dst, tab_sem.at[i])
+        for i, (src, dst) in enumerate(
+            ((kept_hbm, kept_v), (home_hbm, home_v), (dest_hbm, dest_v), (stay_hbm, kept))
+        )
+    ]
+    for copy in tables:
+        copy.start()
     load_q.start()
     load_new.start()
+    load_q.wait()
+    for row in range(PER_GROUP):
+        for h in range(HB):
+            piece = q_in[row, :, h * HD : (h + 1) * HD]
+            stage[row, h * STEPS : (h + 1) * STEPS, :] = piece.astype(F32)
+    for j in range(RES_DEV):
+        qall[t, j] = stage[j].astype(BF16)
+    meet()
+    for j in range(RES_DEV):
+        send_own(j)
+    for copy in tables:
+        copy.wait()
     load_pre.start()
     load_res.start()
-    fill_table(G, g, kept_v, home_v, dest_v, tab_v)
+    sources = [from_g(k) for k in range(G)]
+    fill_table([peer_g(k) for k in range(G)], sources, g, kept_v, home_v, dest_v, tab_v)
     load_tab = pltpu.make_async_copy(tab_v, tab_s, cache_sem.at[4])
     load_tab.start()
     load_tab.wait()
-    load_q.wait()
-
-    def arranged(row, slot):
-        for h in range(HB):
-            piece = q_in[row, :, h * HD : (h + 1) * HD]
-            stage[slot, h * STEPS : (h + 1) * STEPS, :] = piece.astype(F32)
-        return stage[slot].astype(BF16)
 
     for k in range(G):
-        block = arranged(tab_s[peer_g(k), 0], k)
+        block = stage[tab_s[k, 0]].astype(BF16)
         zq[k] = block
-        if k == 0:
-            qall[t, RES_DEV] = block
-    for j in range(RES_DEV):
-        qall[t, j] = arranged(j, G + j)
-
-    pl.semaphore_wait(barrier, G - 1 + T - 1)
-    for k in range(1, G):
-        c_zq(k).start()
-    for n in range(1, T):
-        c_rq(n).start()
-    for n in range(1, T):
-        c_fwd(0, n).start()
-
-    load_new.wait()
+        if k == mine:
+            qall[t, RES_DEV + k] = block
+
+    send_own(RES_DEV + mine)
+    for k in moving:
+        when_below(k, c_zq(k).start)
+
     kv_col = pl.multiple_of((t * KVL * KVH) // (T * KVL) * HD, HD)
-    for b in range(NB):
+
+    def stage_new(b):
         for j in range(BATCH):
-            row = j if b == 0 else tab_s[peer_g((b - 1) * BATCH + j), 0]
+            row = j if b == 0 else tab_s[(b - 1) * BATCH + j, 0]
             lo = j * STEPS
             newk[b, 0, lo : lo + STEPS, :] = new_in[row, :, pl.ds(kv_col, KVL * HD)].astype(F32)
             newk[b, 1, lo : lo + STEPS, :] = new_in[
@@ -223,7 +313,8 @@
     r16 = lax.broadcasted_iota(jnp.int32, (BATCH * STEPS, LW), 0)
     lanes16 = lax.broadcasted_iota(jnp.int32, (BATCH * STEPS, LW), 1)
     causal = (r16 // STEPS == lanes16 // R) & (r16 % STEPS <= lanes16 % STEPS)
-    for b in range(NB):
+    def fresh(b):
+        stage_new(b)
         asked_b = queries_of(b)
         for i in range(KVL):
             keys = newk[b, 0, :, i * HD : (i + 1) * HD].astype(BF16)
@@ -238,12 +329,12 @@
                 weights.astype(BF16), values, TN, preferred_element_type=F32
             )
 
-    for k in range(1, G):
+
+    def forward(k):
         c_zq(k).wait_recv()
-        for n in range(1, T):
-            c_fwd(k, n).start()
-
-    def attend_slot(cache, row, length, slot, b, j):
+        send_own(RES_DEV + k)
+
+    def attend_slot(cache, row, length, slot, b, j, hold=False):
         lane = lax.broadcasted_iota(jnp.int32, (R, 128), 1)
         usable = offset + lax.broadcasted_iota(jnp.int32, (R, pos), 1) < length
         stat = jnp.zeros((R, 128), F32)
@@ -282,43 +373,83 @@
                     w * R : (w + 1) * R, w * HD : (w + 1) * HD
                 ].astype(BF16)
         statbuf[rows, :] = stat
-        for n in range(1, T):
-            c_o(b, j, n).start()
-
-    def send_batch(b):
-        turned = statbuf[...].T
-        for tt in range(T):
-            sbuf[b, tt] = turned[tt * SW : tt * SW + 8, :]
+        if not hold:
+            for n in range(1, T):
+                c_o(b, j, n).start()
+
+    def send_stats(b):
         for n in range(1, T):
             c_st(b, n).start()
         rbuf[b, 0] = obuf[b, t]
         rstat[b, 0] = sbuf[b, t]
 
     rest = pl.ds(1, T - 1)
-    load_pre.wait()
-
-    @pl.loop(1, NB)
-    def _(b):
-        @pl.loop(0, BATCH)
+
+    def loaded(_):
+        load_pre.wait()
+        load_res.wait()
+
+    few = 2 if relay else T - 1
+
+    def stay_slots(first, last, hold):
+        @pl.loop(first, last)
+        def _(j):
+            whole(j, few)
+            attend_slot(res, j, kept[0, g * RES_DEV + j], j, 0, j, hold)
+
+    def moved_slots(b, first, last, came):
+        @pl.loop(first, last)
         def _(j):
             k = (b - 1) * BATCH + j
-            spread = qall.at[rest, RES_DEV + k]
-            over_t(spread, spread, f_s.at[0], f_r.at[k], t).wait_recv()
-            source = from_g(k)
-            held = tab_s[G + source, 0]
+            whole(RES_DEV + k, came)
+            held = tab_s[G + k, 0]
             attend_slot(pre, held % MIG_DEV, held // MIG_DEV, RES_DEV + k, b, j)
 
-        send_batch(b)
-
-    load_res.wait()
-    q_rest = qall.at[rest, pl.ds(0, RES_DEV)]
-    over_t(q_rest, q_rest, rq_s.at[0], rq_r.at[0], t).wait_recv()
-
-    @pl.loop(0, RES_DEV)
-    def _(j):
-        attend_slot(res, j, kept[g * RES_DEV + j], j, 0, j)
-
-    send_batch(0)
+    def turn_stats(b):
+        turned = statbuf[...].T
+        for tt in range(T):
+            sbuf[b, tt] = turned[tt * SW : tt * SW + 8, :]
+
+    def attend_batch(b):
+        moved_slots(b, 0, BATCH, T - 1)
+        turn_stats(b)
+        send_stats(b)
+
+    def attend_first(_):
+        attend_batch(1)
+
+    def attend_rest(_):
+        if NB > 3:
+            pl.loop(2, NB - 1)(attend_batch)
+        moved_slots(NB - 1, 0, BATCH - 2, T - 1)
+        moved_slots(NB - 1, BATCH - 2, BATCH, few)
+        turn_stats(NB - 1)
+        send_stats(NB - 1)
+
+    def send_stays(_):
+        for j in range(RES_DEV):
+            for n in range(1, T):
+                c_o(0, j, n).start()
+        send_stats(0)
+
+    def passing(k):
+        pass_on(RES_DEV + k)
+
+    F, W, N, L, PS = forward, passing, fresh, late, pass_on
+    load_new.wait()
+    middle = list(range(4, beside))
+    def reach(_):
+        if relay:
+            pl.semaphore_wait(across.at[0], 1)
+
+    plan = [(L, beside), (N, 0), (L, 0), (L, 1), (F, beside), (N, 1)]
+    plan += [(PS, j) for j in range(RES_DEV)] + [(W, mine)]
+    plan += [(L, k) for k in middle] + [(reach, 0), (L, 2), (L, 3)]
+    plan += [(F, 0), (F, 1), (W, beside)] + [(F, k) for k in middle] + [(F, 2), (F, 3)] + [(N, b) for b in range(2, NB)] + [(loaded, 0), (lambda _: stay_slots(0, RES_DEV, True), 0)]
+    plan += [(turn_stats, 0), (attend_first, 0), (attend_rest, 0), (send_stays, 0)]
+    for step, p in plan:
+        step(p)
+
     def merged(b):
         over_t(rstat.at[b, rest], rstat.at[b, rest], st_s.at[b], st_r.at[b], t).wait_recv()
         over_t(rbuf.at[b, rest], rbuf.at[b, rest], o_s.at[b], o_r.at[b], t).wait_recv()
@@ -366,12 +497,12 @@
             k = (b - 1) * BATCH + j
             for i in range(KVL):
                 zo[k, i] = blended[i][j * R : (j + 1) * R].astype(BF16)
-            if k:
+            if k != mine:
                 c_zs(k).start()
                 c_zo(k).start()
             else:
-                zrs[0] = zs[0]
-                zro[0] = zo[0]
+                zrs[k] = zs[b - 1]
+                zro[k] = zo[k]
 
     finish(0, *merged(0))
     for j in range(RES_DEV):
@@ -381,7 +512,7 @@
         lanes = lax.broadcasted_iota(jnp.int32, (8, LW), 1)
         stats = jnp.zeros((8, LW), F32)
         first = (b - 1) * BATCH
-        came = pl.ds(max(first, 1), first + BATCH - max(first, 1))
+        came = pl.ds(first, BATCH - (first <= mine < first + BATCH))
         over_g(zrs.at[came], zrs.at[came], zs_s.at[0], zs_r.at[b - 1], g).wait_recv()
         over_g(zro.at[came], zro.at[came], zo_s.at[0], zo_r.at[b - 1], g).wait_recv()
         for j in range(BATCH):
@@ -396,18 +527,16 @@
         finish(b, stats[:KVL], stats[KVL:SW], blended)
     for l in range(MIG_DEV):
         k_of = 0
-        for k in range(1, G):
-            k_of = jnp.where(tab_s[peer_g(k), 0] == RES_DEV + l, k, k_of)
+        for k in range(G):
+            k_of = jnp.where(tab_s[k, 0] == RES_DEV + l, k, k_of)
         put(RES_DEV + k_of, RES_DEV + l)
 
     others = pl.ds(1, G - 1)
     over_g(zq.at[others], zq.at[others], zq_s.at[0], zq_r.at[0], g).wait_send()
     over_g(zrs.at[others], zrs.at[others], zs_s.at[0], zs_r.at[0], g).wait_send()
     over_g(zo.at[others], zo.at[others], zo_s.at[0], zo_r.at[0], g).wait_send()
-    over_t(q_rest, q_rest, rq_s.at[0], rq_r.at[0], t).wait_send()
-    passed = qall.at[0, pl.ds(RES_DEV, G)]
-    for n in range(1, T):
-        over_t(passed, passed, f_s.at[n], f_r.at[0], t).wait_send()
+    sent = qall.at[pl.ds(0, T - 1)]
+    over_t(sent, sent, q_s.at[0], q_r2.at[0], t).wait_send()
     for b in range(NB):
         over_t(rstat.at[b, rest], rstat.at[b, rest], st_s.at[b], st_r.at[b], t).wait_send()
         over_t(rbuf.at[b, rest], rbuf.at[b, rest], o_s.at[b], o_r.at[b], t).wait_send()
@@ -433,14 +562,17 @@
     NB = 1 + G // BATCH
     dma = pltpu.SemaphoreType.DMA
     vmem = pl.BlockSpec(memory_space=pltpu.VMEM)
-    smem = pl.BlockSpec(memory_space=pltpu.SMEM)
     hbm = pl.BlockSpec(memory_space=pl.ANY)
     return pl.pallas_call(
         functools.partial(kernel, G, T),
         out_shape=pltpu.VMEM(queries.shape, BF16),
-        in_specs=[vmem, vmem, vmem, smem, hbm, hbm, hbm, hbm],
+        in_specs=[hbm] * 8,
         out_specs=vmem,
         scratch_shapes=[
+            pltpu.VMEM((1, kept_tokens.shape[0]), jnp.int32),
+            pltpu.VMEM((1, prefill_slot.shape[0]), jnp.int32),
+            pltpu.VMEM((1, decode_slot.shape[0]), jnp.int32),
+            pltpu.SMEM((1, resident_kept.shape[0]), jnp.int32),
             pltpu.VMEM((2 * G, 128), jnp.int32),
             pltpu.SMEM((2 * G, 128), jnp.int32),
             pltpu.VMEM(queries.shape, BF16),
@@ -449,7 +581,7 @@
             pltpu.VMEM(prefill_cache.shape, BF16),
             pltpu.VMEM((T, RES_DEV + G, RB, HD), BF16),
             pltpu.VMEM((G, RB, HD), BF16),
-            pltpu.VMEM((G + RES_DEV, RB, HD), F32),
+            pltpu.VMEM((PER_GROUP, RB, HD), F32),
             pltpu.VMEM((NB, T, KVL, LW, HD), BF16),
             pltpu.VMEM((NB, T, KVL, LW, HD), BF16),
             pltpu.VMEM((NB, T, 8, LW), F32),
@@ -465,12 +597,14 @@
             pltpu.VMEM((NB, KVL, LW, HD), F32),
             pltpu.VMEM((NB * BATCH, RB, HD), F32),
             dma((5,)),
+            dma((4,)),
+            pltpu.SemaphoreType.REGULAR((G,)),
+            pltpu.SemaphoreType.REGULAR((1,)),
             dma((1,)),
             dma((G,)),
             dma((1,)),
-            dma((1,)),
-            dma((T,)),
-            dma((G,)),
+            dma((RES_DEV + G,)),
+            dma((RES_DEV + G,)),
             dma((NB,)),
             dma((NB,)),
             dma((NB,)),
@@ -485,7 +619,7 @@
         kept_tokens[None],
         prefill_slot[None],
         decode_slot[None],
-        resident_kept,
+        resident_kept[None],
         queries, new_entries, resident_cache, prefill_cache)
 
 

time: 29.4 us -> 28.1 us (0.956)
  Pallas kernels: 28.6 us -> 27.3 us
    pallas_call x1, Pallas kernels: 28.6 us -> 27.3 us  [body(): pl.pallas_call(functools.partial(kernel, G, T), out_shape=pltpu.VMEM(quer...]
where the time goes in v1:
time: 28.1 us; the launch traced here: 28 us
  Pallas kernels  27.3 us (97%)
  local copies, waits for them, and re-layouts  0.68 us (2%)
    pallas_call x1, Pallas kernels, body(): pl.pallas_call(functools.partial(kernel, G, T), out_shape=pltpu.VMEM(quer...  27.3 us
    unnamed x1, local copies, waits for them, and re-layouts  0.68 us

profile of v1, /device:TPU:0, one launch (start us, length us, event | category | flops | bytes accessed | tf_op | source)
XLA Modules:
  0.0 28.0 jit_solution(9680202758610711259)
XLA Ops:
  0.0 27.3 %shard_map.82 = bf16[12,4,2048]{2,1,0:T(4,128)(2,1)S(1)} custom-call(s32[1,64]{1,0:T(1,128)} %bitcast.4, s32[1,64]{1,0:T(1,128)} %bitcast.5, s32[1,64]{1,0:T(1,128)} %bitcast.6, s32[1,32]{1,0:T(1,128)} %bitcast.7, bf16[12,4,2048]{2,1,0:T(4,128)(2,1)} %q_hbm.1, bf16[12,4,2048]{2,1,0:T(4,128)(2,1)} %new_hbm.1, bf16[4,128,2048]{2,1,0:T(8,128)(2,1)} %res_hbm.1, ...), custom_call_target="tpu_custom_call" | custom-call | tf_op jit(solution)/shard_map/pallas_call | solution.py:566
  27.3 0.7 %copy.10 = bf16[12,4,2048]{2,1,0:T(4,128)(2,1)} copy(bf16[12,4,2048]{2,1,0:T(4,128)(2,1)S(1)} %shard_map.82) | data formatting | bytes 393216

commit v2 on v1

v2 whole, which is shorter than its diff:
```python
import functools
import math

import jax
import jax.numpy as jnp
from jax import lax
from jax.experimental import pallas as pl
from jax.experimental.pallas import tpu as pltpu
from jax.sharding import PartitionSpec as P

H = 64
KVH = 8
HD = 128
STEPS = 4
MIG_DEV = 8
RES_DEV = 4
PER_GROUP = RES_DEV + MIG_DEV
BATCH = 2
STAY = RES_DEV // BATCH

NEG_FLOOR = -1e30
SCALE = 1.0 / math.sqrt(HD)
MESH = pl.DeviceIdType.MESH
F32 = jnp.float32
BF16 = jnp.bfloat16
NT = (((1,), (1,)), ((), ()))
TN = (((0,), (0,)), ((), ()))


def flipped(v, mask):
    out, bit = v, 1
    while bit <= mask:
        if mask & bit:
            out = out + bit * (1 - 2 * lax.rem(lax.div(v, bit), 2))
        bit *= 2
    return out


def fill_table(peers, sources, g, kept_v, home_v, dest_v, tab_v):
    G = len(peers)
    shape = (2 * G, dest_v.shape[1])
    n = lax.broadcasted_iota(jnp.int32, shape, 0)
    dest = jnp.broadcast_to(dest_v[...], shape)
    home = jnp.broadcast_to(home_v[...], shape)
    kept = jnp.broadcast_to(kept_v[...], shape)
    dest_group, home_group = lax.div(dest, PER_GROUP), lax.div(home, MIG_DEV)
    other = jnp.zeros(shape, jnp.int32)
    for k in range(G):
        other = jnp.where(n == k, peers[k], other)
        other = jnp.where(n == G + k, sources[k], other)
    arriving = (n < G) & (dest_group == g) & (home_group == other)
    leaving = (n >= G) & (home_group == g) & (dest_group == other)
    picked = jnp.where(arriving, dest - dest_group * PER_GROUP, 0)
    held = home - home_group * MIG_DEV + MIG_DEV * kept
    picked = picked + jnp.where(leaving, held, 0)
    total = jnp.sum(picked, axis=1, keepdims=True)
    tab_v[...] = jnp.broadcast_to(total, tab_v.shape)


def kernel(
    G,
    T,
    kept_hbm,
    home_hbm,
    dest_hbm,
    stay_hbm,
    q_hbm,
    new_hbm,
    res_hbm,
    pre_hbm,
    out,
    kept_v,
    home_v,
    dest_v,
    kept,
    tab_v,
    tab_s,
    q_in,
    new_in,
    res,
    pre,
    qall,
    zq,
    stage,
    obuf,
    rbuf,
    sbuf,
    rstat,
    statbuf,
    facbuf,
    zo,
    zro,
    zs,
    zrs,
    newk,
    nstat,
    nadd,
    fin,
    cache_sem,
    tab_sem,
    above,
    across,
    zq_s,
    zq_r,
    q_s,
    q_r,
    o_s,
    o_r,
    st_s,
    st_r,
    zo_s,
    zo_r,
    zs_s,
    zs_r,
):
    KVL = max(1, KVH // T)
    HB = H // T
    HU = HB // KVL
    R = STEPS * HU
    LW = BATCH * R
    PW = KVL * LW
    NB = STAY + G // BATCH
    pos = res.shape[1]
    half = KVH * HD
    g = lax.axis_index("group")
    t = lax.axis_index("tensor")
    offset = t * pos

    def peer_t(k):
        return lax.rem(t + k, T)

    paired = G & (G - 1) == 0
    square = T == 4
    row_dev = t + 1 - 2 * lax.rem(t, 2)
    col_dev = t + 2 - 4 * lax.div(t, 2)
    greeted = (row_dev, col_dev, T - 1 - t) if square else [lax.rem(t + n, T) for n in range(1, T)]

    far_pairs = G // 2 - 1
    mine, beside = G - 1, G - 2

    def way(k):
        static = isinstance(k, int)
        if static and k >= beside:
            return mine - k
        pair = k // 2 if static else lax.div(k, 2)
        odd = k % 2 if static else lax.rem(k, 2)
        return 2 * (far_pairs - pair) + odd

    def at_way(mask):
        if not paired:
            return lax.rem(g + mask, G)
        out, bit = 0, 1
        while bit < G:
            a = lax.rem(lax.div(g, bit), 2)
            b = mask // bit % 2 if isinstance(mask, int) else lax.rem(lax.div(mask, bit), 2)
            out = out + bit * (a + b - 2 * a * b)
            bit *= 2
        return out

    def peer_g(k):
        return at_way(way(k))

    def from_g(k):
        return peer_g(k) if paired else at_way(G - way(k))

    level = lax.div(g, 2)
    first = far_pairs - lax.max(level, 1)

    def turn(i):
        if not paired:
            return i
        later = i - 1 + jnp.where(i > first, 1, 0)
        return jnp.where(i == 0, first, later)

    def turn_in(i):
        return jnp.where(first == far_pairs - 1, i, turn(i)) if paired else i

    def over_t(src, dst, ssem, rsem, dev):
        return pltpu.make_async_remote_copy(
            src_ref=src, dst_ref=dst, send_sem=ssem, recv_sem=rsem,
            device_id=(g, dev), device_id_type=MESH,
        )

    def over_g(src, dst, ssem, rsem, dev):
        return pltpu.make_async_remote_copy(
            src_ref=src, dst_ref=dst, send_sem=ssem, recv_sem=rsem,
            device_id=(dev, t), device_id_type=MESH,
        )

    def c_zq(k):
        return over_g(zq.at[k], qall.at[t, RES_DEV + k], zq_s.at[0], zq_r.at[k], peer_g(k))

    near = greeted[:2] if square else greeted

    def send_own(s, devs):
        own = qall.at[t, s]
        for dev in devs:
            over_t(own, own, q_s.at[0], q_r.at[s], dev).start()

    def whole(s):
        rest = qall.at[pl.ds(0, T - 1), s]
        over_t(rest, rest, q_s.at[0], q_r.at[s], t).wait_recv()

    def c_o(b, j, n):
        p = peer_t(n)
        rows = pl.ds(pl.multiple_of(j * R, R), R)
        return over_t(
            obuf.at[b, p, :, rows], rbuf.at[b, n, :, rows], o_s.at[0], o_r.at[b], p
        )

    def c_st(b, n):
        p = peer_t(n)
        return over_t(sbuf.at[b, p], rstat.at[b, n], st_s.at[0], st_r.at[b], p)

    barrier = pltpu.get_barrier_semaphore()
    moving = [k for k in range(G) if k != mine]

    def when_above(k, act):
        @pl.when(peer_g(k) > g)
        def _():
            act()

    def when_below(k, act):
        @pl.when(peer_g(k) < g)
        def _():
            act()

    def greet(k):
        pl.semaphore_signal(barrier, inc=1, device_id=(peer_g(k), t), device_id_type=MESH)

    def answer(k):
        back = k if paired else [way(m) for m in range(G)].index((G - way(k)) % G)
        pl.semaphore_signal(
            above.at[back], inc=1, device_id=(peer_g(k), t), device_id_type=MESH
        )

    def send_up(k):
        pl.semaphore_wait(above.at[k], 1)
        c_zq(k).start()

    def late(k):
        when_above(k, functools.partial(send_up, k))

    def meet():
        pl.semaphore_wait(barrier, g + len(near))
        for k in moving:
            when_below(k, functools.partial(answer, k))
        if square:
            pl.semaphore_signal(
                across.at[0], inc=1, device_id=(g, row_dev), device_id_type=MESH
            )

    for k in moving:
        when_above(k, functools.partial(greet, k))
    for dev in near:
        pl.semaphore_signal(barrier, inc=1, device_id=(g, dev), device_id_type=MESH)
    load_q = pltpu.make_async_copy(q_hbm, q_in, cache_sem.at[2])
    load_new = pltpu.make_async_copy(new_hbm, new_in, cache_sem.at[3])
    load_res = pltpu.make_async_copy(res_hbm, res, cache_sem.at[0])
    load_pre = pltpu.make_async_copy(pre_hbm, pre, cache_sem.at[1])
    tables = [
        pltpu.make_async_copy(src, dst, tab_sem.at[i])
        for i, (src, dst) in enumerate(
            ((kept_hbm, kept_v), (home_hbm, home_v), (dest_hbm, dest_v), (stay_hbm, kept))
        )
    ]
    for copy in tables:
        copy.start()
    load_q.start()
    load_new.start()
    load_q.wait()
    for row in range(PER_GROUP):
        for h in range(HB):
            piece = q_in[row, :, h * HD : (h + 1) * HD]
            stage[row, h * STEPS : (h + 1) * STEPS, :] = piece.astype(F32)
    for j in range(RES_DEV):
        qall[t, j] = stage[j].astype(BF16)
    meet()
    for j in range(RES_DEV):
        send_own(j, near)
    for copy in tables:
        copy.wait()
    load_pre.start()
    load_res.start()
    sources = [from_g(k) for k in range(G)]
    fill_table([peer_g(k) for k in range(G)], sources, g, kept_v, home_v, dest_v, tab_v)
    load_tab = pltpu.make_async_copy(tab_v, tab_s, cache_sem.at[4])
    load_tab.start()
    load_tab.wait()

    for k in range(G):
        block = stage[tab_s[k, 0]].astype(BF16)
        zq[k] = block
        if k == mine:
            qall[t, RES_DEV + k] = block

    for k in reversed(moving):
        when_below(k, c_zq(k).start)
    send_own(RES_DEV + mine, near)

    kv_col = pl.multiple_of((t * KVL * KVH) // (T * KVL) * HD, HD)

    def stage_new(b):
        for j in range(BATCH):
            row = b * BATCH + j if b < STAY else tab_s[(b - STAY) * BATCH + j, 0]
            for c in range(2):
                for i in range(KVL):
                    lo = (i * BATCH + j) * STEPS
                    col = pl.multiple_of(c * half + kv_col + i * HD, HD)
                    newk[b, c, lo : lo + STEPS, :] = new_in[row, :, pl.ds(col, HD)].astype(F32)

    def asked_of(b, j):
        return qall[t, b * BATCH + j] if b < STAY else zq[(b - STAY) * BATCH + j]

    r16 = lax.broadcasted_iota(jnp.int32, (KVL * BATCH * STEPS, PW), 0)
    lanes16 = lax.broadcasted_iota(jnp.int32, (KVL * BATCH * STEPS, PW), 1)
    causal = (r16 // STEPS == lanes16 // R) & (r16 % STEPS <= lanes16 % STEPS)

    def fresh(b):
        stage_new(b)
        asked = jnp.concatenate(
            [asked_of(b, j)[i * R : (i + 1) * R] for i in range(KVL) for j in range(BATCH)],
            axis=0,
        )
        keys, values = newk[b, 0].astype(BF16), newk[b, 1].astype(BF16)
        scores = lax.dot_general(keys, asked, NT, preferred_element_type=F32) * SCALE
        scores = jnp.where(causal, scores, NEG_FLOOR)
        top = jnp.max(scores, axis=0, keepdims=True)
        weights = jnp.where(causal, jnp.exp(scores - top), 0.0)
        nstat[b, 0:1, :] = top
        nstat[b, 1:2, :] = jnp.sum(weights, axis=0, keepdims=True)
        nadd[b] = lax.dot_general(
            weights.astype(BF16), values, TN, preferred_element_type=F32
        )

    def forward(k):
        came = qall.at[t, RES_DEV + k]
        over_g(came, came, zq_s.at[0], zq_r.at[k], g).wait_recv()
        send_own(RES_DEV + k, greeted)

    def attend_slot(cache, row, length, slot, b, j, hold=False):
        lane = lax.broadcasted_iota(jnp.int32, (R, 128), 1)
        usable = offset + lax.broadcasted_iota(jnp.int32, (R, pos), 1) < length
        stats = [jnp.zeros((R, 128), F32) for _ in range(KVL)]
        rows = pl.ds(pl.multiple_of(j * R, R), R)
        W = 2 if KVL % 2 == 0 else 1
        units = [(tt, i) for tt in range(T) for i in range(0, KVL, W)]
        all_scores = []
        for tt, i in units:
            kv = (tt * KVL + i) * KVH // (T * KVL)
            asked = qall[tt, slot, i * R : (i + W) * R, :]
            keys = jnp.concatenate(
                [cache[row, :, (kv + w) * HD : (kv + w + 1) * HD] for w in range(W)], axis=0
            )
            scores = lax.dot_general(asked, keys, NT, preferred_element_type=F32)
            all_scores.append(
                [scores[w * R : (w + 1) * R, w * pos : (w + 1) * pos] * SCALE for w in range(W)]
            )
        all_weights = []
        for (tt, i), scores in zip(units, all_scores):
            rounded = []
            for w in range(W):
                masked = jnp.where(usable, scores[w], NEG_FLOOR)
                highest = jnp.max(masked, axis=1, keepdims=True)
                weights = jnp.where(usable, jnp.exp(masked - highest), 0.0)
                total = jnp.sum(weights, axis=1, keepdims=True)
                rounded.append(weights.astype(BF16))
                stats[i + w] = jnp.where(lane == 2 * tt, highest, stats[i + w])
                stats[i + w] = jnp.where(lane == 2 * tt + 1, total, stats[i + w])
            all_weights.append(jnp.concatenate(rounded, axis=0))
        for (tt, i), weights in zip(units, all_weights):
            kv = (tt * KVL + i) * KVH // (T * KVL)
            values = cache[row, :, half + kv * HD : half + (kv + W) * HD]
            blended = jnp.dot(weights, values, preferred_element_type=F32)
            for w in range(W):
                obuf[b, tt, i + w, rows, :] = blended[
                    w * R : (w + 1) * R, w * HD : (w + 1) * HD
                ].astype(BF16)
        for i in range(KVL):
            statbuf[pl.ds(pl.multiple_of(i * LW + j * R, R), R), :] = stats[i]
        if not hold:
            for n in range(1, T):
                c_o(b, j, n).start()

    def send_stats(b):
        for n in range(1, T):
            c_st(b, n).start()
        rbuf[b, 0] = obuf[b, t]
        rstat[b, 0] = sbuf[b, t]

    rest = pl.ds(1, T - 1)

    def loaded(_):
        load_pre.wait()
        load_res.wait()

    def turn_stats(b):
        turned = statbuf[...].T
        for tt in range(T):
            sbuf[b, tt] = turned[2 * tt : 2 * tt + 2, :]

    def stay_batch(b, hold=True):
        @pl.loop(0, BATCH)
        def _(j):
            s = b * BATCH + j
            whole(s)
            attend_slot(res, s, kept[0, g * RES_DEV + s], s, b, j, hold)

        turn_stats(b)
        if not hold:
            send_stats(b)

    def moved_batch(b, hold=False):
        @pl.loop(0, BATCH)
        def _(j):
            k = (b - STAY) * BATCH + j
            whole(RES_DEV + k)
            held = tab_s[G + k, 0]
            attend_slot(pre, held % MIG_DEV, held // MIG_DEV, RES_DEV + k, b, j, hold)

        turn_stats(b)
        if not hold:
            send_stats(b)

    def send_batch(b):
        for j in range(BATCH):
            for n in range(1, T):
                c_o(b, j, n).start()
        send_stats(b)

    def reach(_):
        if square:
            pl.semaphore_wait(across.at[0], 1)
            for s in (*range(RES_DEV), RES_DEV + mine):
                send_own(s, greeted[2:])

    def stays():
        pl.loop(0, STAY)(stay_batch)

    def locals_held(_):
        moved_batch(NB - 1, True)

    def far(_):
        @pl.loop(0, far_pairs)
        def _(i):
            moved_batch(STAY + turn(i))

    def forward_far(_):
        @pl.loop(0, far_pairs - 1)
        def _(i):
            for j in range(2):
                forward(2 * turn_in(i) + j)


    F, N, L = forward, fresh, late
    load_new.wait()
    middle = list(range(2, beside))
    early = g < G // 4

    def stays_early(_):
        @pl.when(early)
        def _():
            stay_batch(0, False)
            pl.loop(1, STAY)(stay_batch)

    def stays_late(_):
        pl.when(jnp.logical_not(early))(stays)

    def held_late(_):
        pl.when(jnp.logical_not(early))(functools.partial(send_batch, 0))
        for b in range(1, STAY):
            send_batch(b)

    plan = [(L, beside), (N, 0), (L, beside - 2), (L, beside - 1), (reach, 0), (F, beside)]
    plan += [(N, 1)] + [(L, k) for k in reversed(range(beside - 2))]
    plan += [(F, beside - 2), (F, beside - 1), (loaded, 0), (stays_early, 0), (N, NB - 1)]
    plan += [(forward_far, 0)]
    plan += [(stays_late, 0), (locals_held, 0), (far, 0), (send_batch, NB - 1)]
    plan += [(held_late, 0)]
    plan += [(N, b) for b in range(STAY, NB - 1)]
    for step, p in plan:
        step(p)

    def arrived(b):
        over_t(rstat.at[b, rest], rstat.at[b, rest], st_s.at[0], st_r.at[b], t).wait_recv()
        over_t(rbuf.at[b, rest], rbuf.at[b, rest], o_s.at[0], o_r.at[b], t).wait_recv()

    def merged(b):
        tops = [rstat[b, n][0:1] for n in range(T)]
        highest = functools.reduce(jnp.maximum, tops)
        total = jnp.zeros((1, PW), F32)
        for n in range(T):
            factor = jnp.exp(tops[n] - highest)
            total = total + factor * rstat[b, n][1:2]
            facbuf[b, n : n + 1, :] = factor
        columns = facbuf[b].T
        blended = jnp.zeros((PW, HD), F32)
        for n in range(T):
            part = rbuf[b, n].reshape(PW, HD).astype(F32)
            blended = blended + part * columns[:, n : n + 1]
        return highest, total, blended

    def finish(b, highest, total, blended):
        new_top, new_total = nstat[b, 0:1], nstat[b, 1:2]
        top = jnp.maximum(highest, new_top)
        old_part, new_part = jnp.exp(highest - top), jnp.exp(new_top - top)
        inverse = 1.0 / (total * old_part + new_total * new_part)
        facbuf[NB + b, 0:1, :] = old_part * inverse
        facbuf[NB + b, 1:2, :] = new_part * inverse
        columns = facbuf[NB + b].T
        done = blended * columns[:, 0:1] + nadd[b] * columns[:, 1:2]
        for j in range(BATCH):
            for i in range(KVL):
                lo = i * LW + j * R
                fin[b * BATCH + j, i * R : (i + 1) * R, :] = done[lo : lo + R]

    def put(slot, row):
        for h in range(HB):
            piece = fin[slot, h * STEPS : (h + 1) * STEPS, :]
            out[row, :, h * HD : (h + 1) * HD] = piece.astype(BF16)

    def give_back(b):
        arrived(b)
        highest, total, blended = merged(b)
        zs[b - STAY] = jnp.concatenate([highest, total], axis=0)
        for j in range(BATCH):
            k = (b - STAY) * BATCH + j
            for i in range(KVL):
                zo[k, i] = blended[i * LW + j * R : i * LW + (j + 1) * R].astype(BF16)
            if isinstance(k, int) and k == mine:
                zrs[k] = zs[b - STAY]
                zro[k] = zo[k]
            else:
                pair, dev = b - STAY, from_g(k)
                over_g(zs.at[pair], zrs.at[k], zs_s.at[0], zs_r.at[pair], dev).start()
                over_g(zo.at[k], zro.at[k], zo_s.at[0], zo_r.at[pair], dev).start()

    def give_far(_):
        @pl.loop(0, far_pairs)
        def _(i):
            give_back(STAY + turn(i))

    def end_stay(b):
        finish(b, *merged(b))
        for j in range(BATCH):
            put(b * BATCH + j, b * BATCH + j)

    def returned(b):
        first = (b - STAY) * BATCH
        came = pl.ds(first, BATCH - (first <= mine < first + BATCH))
        over_g(zrs.at[came], zrs.at[came], zs_s.at[0], zs_r.at[b - STAY], g).wait_recv()
        over_g(zro.at[came], zro.at[came], zo_s.at[0], zo_r.at[b - STAY], g).wait_recv()

    def end_moved(b):
        lanes = lax.broadcasted_iota(jnp.int32, (2, PW), 1)
        stats = jnp.zeros((2, PW), F32)
        first = (b - STAY) * BATCH
        for j in range(BATCH):
            stats = jnp.where((lanes // R) % BATCH == j, zrs[first + j], stats)
        blended = jnp.concatenate(
            [zro[first + j, i].astype(F32) for i in range(KVL) for j in range(BATCH)], axis=0
        )
        finish(b, stats[0:1], stats[1:2], blended)

    moved = list(range(STAY, NB))
    def stay_early(_):
        @pl.when(early)
        def _():
            arrived(0)
            end_stay(0)

    def stay_late(_):
        @pl.when(jnp.logical_not(early))
        def _():
            arrived(0)
            end_stay(0)

    plan = [(stay_early, 0), (give_far, 0), (give_back, moved[-1]), (stay_late, 0)]
    plan += [(returned, b) for b in moved] + [(end_moved, b) for b in moved]
    for b in range(1, STAY):
        plan += [(arrived, b), (end_stay, b)]
    for step, p in plan:
        step(p)
    for l in range(MIG_DEV):
        k_of = 0
        for k in range(G):
            k_of = jnp.where(tab_s[k, 0] == RES_DEV + l, k, k_of)
        put(RES_DEV + k_of, RES_DEV + l)

    others = pl.ds(1, G - 1)
    over_g(zq.at[others], zq.at[others], zq_s.at[0], zq_r.at[0], g).wait_send()
    over_g(zrs.at[others], zrs.at[others], zs_s.at[0], zs_r.at[0], g).wait_send()
    over_g(zo.at[others], zo.at[others], zo_s.at[0], zo_r.at[0], g).wait_send()
    sent = qall.at[pl.ds(0, T - 1)]
    over_t(sent, sent, q_s.at[0], q_r.at[0], t).wait_send()
    stats, parts = rstat.at[:, rest], rbuf.at[:, rest]
    over_t(stats, stats, st_s.at[0], st_r.at[0], t).wait_send()
    over_t(parts, parts, o_s.at[0], o_r.at[0], t).wait_send()


def body(
    queries,
    new_entries,
    resident_cache,
    prefill_cache,
    resident_kept,
    kept_tokens,
    prefill_slot,
    decode_slot,
):
    G = lax.axis_size("group")
    T = lax.axis_size("tensor")
    KVL = max(1, KVH // T)
    HB = H // T
    RB = STEPS * HB
    R = RB // KVL
    LW = BATCH * R
    NB = STAY + G // BATCH
    PW = KVL * LW
    dma = pltpu.SemaphoreType.DMA
    vmem = pl.BlockSpec(memory_space=pltpu.VMEM)
    hbm = pl.BlockSpec(memory_space=pl.ANY)
    return pl.pallas_call(
        functools.partial(kernel, G, T),
        out_shape=pltpu.VMEM(queries.shape, BF16),
        in_specs=[hbm] * 8,
        out_specs=vmem,
        scratch_shapes=[
            pltpu.VMEM((1, kept_tokens.shape[0]), jnp.int32),
            pltpu.VMEM((1, prefill_slot.shape[0]), jnp.int32),
            pltpu.VMEM((1, decode_slot.shape[0]), jnp.int32),
            pltpu.SMEM((1, resident_kept.shape[0]), jnp.int32),
            pltpu.VMEM((2 * G, 128), jnp.int32),
            pltpu.SMEM((2 * G, 128), jnp.int32),
            pltpu.VMEM(queries.shape, BF16),
            pltpu.VMEM(new_entries.shape, BF16),
            pltpu.VMEM(resident_cache.shape, BF16),
            pltpu.VMEM(prefill_cache.shape, BF16),
            pltpu.VMEM((T, RES_DEV + G, RB, HD), BF16),
            pltpu.VMEM((G, RB, HD), BF16),
            pltpu.VMEM((PER_GROUP, RB, HD), F32),
            pltpu.VMEM((NB, T, KVL, LW, HD), BF16),
            pltpu.VMEM((NB, T, KVL, LW, HD), BF16),
            pltpu.VMEM((NB, T, 2, PW), F32),
            pltpu.VMEM((NB, T, 2, PW), F32),
            pltpu.VMEM((PW, 128), F32),
            pltpu.VMEM((2 * NB, max(8, T), PW), F32),
            pltpu.VMEM((G, KVL, R, HD), BF16),
            pltpu.VMEM((G, KVL, R, HD), BF16),
            pltpu.VMEM((NB - STAY, 2, PW), F32),
            pltpu.VMEM((G, 2, PW), F32),
            pltpu.VMEM((NB, 2, KVL * BATCH * STEPS, HD), F32),
            pltpu.VMEM((NB, 2, PW), F32),
            pltpu.VMEM((NB, PW, HD), F32),
            pltpu.VMEM((NB * BATCH, RB, HD), F32),
            dma((5,)),
            dma((4,)),
            pltpu.SemaphoreType.REGULAR((G,)),
            pltpu.SemaphoreType.REGULAR((1,)),
            dma((1,)),
            dma((G,)),
            dma((1,)),
            dma((RES_DEV + G,)),
            dma((1,)),
            dma((NB,)),
            dma((1,)),
            dma((NB,)),
            dma((1,)),
            dma((NB - STAY,)),
            dma((1,)),
            dma((NB - STAY,)),
        ],
        compiler_params=pltpu.CompilerParams(collective_id=0, has_side_effects=True),
    )(
        kept_tokens[None],
        prefill_slot[None],
        decode_slot[None],
        resident_kept[None],
        queries, new_entries, resident_cache, prefill_cache)


def solution(mesh):
    in_specs = (
        P("group", None, "tensor"),
        P("group", None, None),
        P("group", "tensor", None),
        P("group", "tensor", None),
        P(),
        P(),
        P(),
        P(),
    )
    out_specs = P("group", None, "tensor")
    return jax.shard_map(body, mesh=mesh, in_specs=in_specs, out_specs=out_specs, check_vma=False)
```

time: 28.1 us -> 25.4 us (0.904)
  Pallas kernels: 27.3 us -> 24.5 us
    pallas_call x1, Pallas kernels: 27.3 us -> 24.5 us  [body(): pl.pallas_call(functools.partial(kernel, G, T), out_shape=pltpu.VMEM(quer...]
where the time goes in v2:
time: 25.4 us; the launch traced here: 25.2 us
  Pallas kernels  24.5 us (96%)
  local copies, waits for them, and re-layouts  0.68 us (3%)
    pallas_call x1, Pallas kernels, body(): pl.pallas_call(functools.partial(kernel, G, T), out_shape=pltpu.VMEM(quer...  24.5 us
    unnamed x1, local copies, waits for them, and re-layouts  0.68 us

profile of v2, /device:TPU:0, one launch (start us, length us, event | category | flops | bytes accessed | tf_op | source)
XLA Modules:
  0.0 25.2 jit_solution(644802537757865180)
XLA Ops:
  0.0 24.5 %shard_map.82 = bf16[12,4,2048]{2,1,0:T(4,128)(2,1)S(1)} custom-call(s32[1,64]{1,0:T(1,128)} %bitcast.4, s32[1,64]{1,0:T(1,128)} %bitcast.5, s32[1,64]{1,0:T(1,128)} %bitcast.6, s32[1,32]{1,0:T(1,128)} %bitcast.7, bf16[12,4,2048]{2,1,0:T(4,128)(2,1)} %q_hbm.1, bf16[12,4,2048]{2,1,0:T(4,128)(2,1)} %new_hbm.1, bf16[4,128,2048]{2,1,0:T(8,128)(2,1)} %res_hbm.1, ...), custom_call_target="tpu_custom_call" | custom-call | tf_op jit(solution)/shard_map/pallas_call | solution.py:623
  24.5 0.7 %copy.10 = bf16[12,4,2048]{2,1,0:T(4,128)(2,1)} copy(bf16[12,4,2048]{2,1,0:T(4,128)(2,1)S(1)} %shard_map.82) | data formatting | bytes 393216

commit v3 on v2

--- a/solution.py
+++ b/solution.py
@@ -36,13 +36,13 @@
     return out
 
 
-def fill_table(peers, sources, g, kept_v, home_v, dest_v, tab_v):
+def fill_table(peers, sources, g, plan_v, tab_v):
     G = len(peers)
-    shape = (2 * G, dest_v.shape[1])
+    shape = (2 * G, plan_v.shape[1])
     n = lax.broadcasted_iota(jnp.int32, shape, 0)
-    dest = jnp.broadcast_to(dest_v[...], shape)
-    home = jnp.broadcast_to(home_v[...], shape)
-    kept = jnp.broadcast_to(kept_v[...], shape)
+    dest = jnp.broadcast_to(plan_v[2:3, :], shape)
+    home = jnp.broadcast_to(plan_v[1:2, :], shape)
+    kept = jnp.broadcast_to(plan_v[0:1, :], shape)
     dest_group, home_group = lax.div(dest, PER_GROUP), lax.div(home, MIG_DEV)
     other = jnp.zeros(shape, jnp.int32)
     for k in range(G):
@@ -69,16 +69,13 @@
     res_hbm,
     pre_hbm,
     out,
-    kept_v,
-    home_v,
-    dest_v,
+    plan_v,
     kept,
     tab_v,
     tab_s,
     q_in,
     new_in,
-    res,
-    pre,
+    cache,
     qall,
     zq,
     stage,
@@ -96,8 +93,7 @@
     nstat,
     nadd,
     fin,
-    cache_sem,
-    tab_sem,
+    load_sem,
     above,
     across,
     zq_s,
@@ -120,20 +116,21 @@
     LW = BATCH * R
     PW = KVL * LW
     NB = STAY + G // BATCH
-    pos = res.shape[1]
+    pos = cache.shape[1]
     half = KVH * HD
     g = lax.axis_index("group")
     t = lax.axis_index("tensor")
     offset = t * pos
 
-    def peer_t(k):
-        return lax.rem(t + k, T)
-
     paired = G & (G - 1) == 0
     square = T == 4
     row_dev = t + 1 - 2 * lax.rem(t, 2)
     col_dev = t + 2 - 4 * lax.div(t, 2)
-    greeted = (row_dev, col_dev, T - 1 - t) if square else [lax.rem(t + n, T) for n in range(1, T)]
+    greeted = (
+        [(3, T - 1 - t), (2, col_dev), (1, row_dev)]
+        if square
+        else [(n, lax.rem(t + n, T)) for n in range(1, T)]
+    )
 
     far_pairs = G // 2 - 1
     mine, beside = G - 1, G - 2
@@ -190,27 +187,28 @@
     def c_zq(k):
         return over_g(zq.at[k], qall.at[t, RES_DEV + k], zq_s.at[0], zq_r.at[k], peer_g(k))
 
-    near = greeted[:2] if square else greeted
+    near = greeted[1:] if square else greeted
 
     def send_own(s, devs):
         own = qall.at[t, s]
-        for dev in devs:
+        for _, dev in devs:
             over_t(own, own, q_s.at[0], q_r.at[s], dev).start()
 
     def whole(s):
         rest = qall.at[pl.ds(0, T - 1), s]
         over_t(rest, rest, q_s.at[0], q_r.at[s], t).wait_recv()
 
-    def c_o(b, j, n):
-        p = peer_t(n)
+    def c_o(b, j, n, p):
         rows = pl.ds(pl.multiple_of(j * R, R), R)
         return over_t(
-            obuf.at[b, p, :, rows], rbuf.at[b, n, :, rows], o_s.at[0], o_r.at[b], p
+            obuf.at[b, p, :, rows], rbuf.at[b, back(n), :, rows], o_s.at[0], o_r.at[b], p
         )
 
-    def c_st(b, n):
-        p = peer_t(n)
-        return over_t(sbuf.at[b, p], rstat.at[b, n], st_s.at[0], st_r.at[b], p)
+    def c_st(b, n, p):
+        return over_t(sbuf.at[b, p], rstat.at[b, back(n)], st_s.at[0], st_r.at[b], p)
+
+    def back(n):
+        return n if square else T - n
 
     barrier = pltpu.get_barrier_semaphore()
     moving = [k for k in range(G) if k != mine]
@@ -231,15 +229,17 @@
     def answer(k):
         back = k if paired else [way(m) for m in range(G)].index((G - way(k)) % G)
         pl.semaphore_signal(
-            above.at[back], inc=1, device_id=(peer_g(k), t), device_id_type=MESH
+            above.at[back // 2 if paired else back], inc=1, device_id=(peer_g(k), t), device_id_type=MESH
         )
 
-    def send_up(k):
-        pl.semaphore_wait(above.at[k], 1)
-        c_zq(k).start()
-
     def late(k):
-        when_above(k, functools.partial(send_up, k))
+        @pl.when(peer_g(k) > g)
+        def _():
+            if not paired:
+                pl.semaphore_wait(above.at[k], 1)
+            elif k % 2 == 0:
+                pl.semaphore_wait(above.at[k // 2], 1 if k == beside else 2)
+            c_zq(k).start()
 
     def meet():
         pl.semaphore_wait(barrier, g + len(near))
@@ -252,39 +252,49 @@
 
     for k in moving:
         when_above(k, functools.partial(greet, k))
-    for dev in near:
+    for _, dev in near:
         pl.semaphore_signal(barrier, inc=1, device_id=(g, dev), device_id_type=MESH)
-    load_q = pltpu.make_async_copy(q_hbm, q_in, cache_sem.at[2])
-    load_new = pltpu.make_async_copy(new_hbm, new_in, cache_sem.at[3])
-    load_res = pltpu.make_async_copy(res_hbm, res, cache_sem.at[0])
-    load_pre = pltpu.make_async_copy(pre_hbm, pre, cache_sem.at[1])
+    load_q = pltpu.make_async_copy(q_hbm, q_in, load_sem.at[2])
+    load_new = pltpu.make_async_copy(new_hbm, new_in, load_sem.at[3])
+    load_pre = pltpu.make_async_copy(pre_hbm, cache.at[0:MIG_DEV], load_sem.at[4])
+    load_res = pltpu.make_async_copy(res_hbm, cache.at[MIG_DEV:PER_GROUP], load_sem.at[4])
     tables = [
-        pltpu.make_async_copy(src, dst, tab_sem.at[i])
+        pltpu.make_async_copy(src, dst, load_sem.at[i // 3])
         for i, (src, dst) in enumerate(
-            ((kept_hbm, kept_v), (home_hbm, home_v), (dest_hbm, dest_v), (stay_hbm, kept))
+            (
+                (kept_hbm, plan_v.at[0:1]),
+                (home_hbm, plan_v.at[1:2]),
+                (dest_hbm, plan_v.at[2:3]),
+                (stay_hbm, kept),
+            )
         )
     ]
     for copy in tables:
         copy.start()
     load_q.start()
     load_new.start()
+    meet()
     load_q.wait()
-    for row in range(PER_GROUP):
+
+    def arrange(row):
         for h in range(HB):
             piece = q_in[row, :, h * HD : (h + 1) * HD]
             stage[row, h * STEPS : (h + 1) * STEPS, :] = piece.astype(F32)
+
     for j in range(RES_DEV):
+        arrange(j)
         qall[t, j] = stage[j].astype(BF16)
-    meet()
     for j in range(RES_DEV):
         send_own(j, near)
-    for copy in tables:
-        copy.wait()
+    for row in range(RES_DEV, PER_GROUP):
+        arrange(row)
+    pltpu.make_async_copy(plan_v, plan_v, load_sem.at[0]).wait()
+    tables[3].wait()
     load_pre.start()
     load_res.start()
     sources = [from_g(k) for k in range(G)]
-    fill_table([peer_g(k) for k in range(G)], sources, g, kept_v, home_v, dest_v, tab_v)
-    load_tab = pltpu.make_async_copy(tab_v, tab_s, cache_sem.at[4])
+    fill_table([peer_g(k) for k in range(G)], sources, g, plan_v, tab_v)
+    load_tab = pltpu.make_async_copy(tab_v, tab_s, load_sem.at[2])
     load_tab.start()
     load_tab.wait()
 
@@ -315,6 +325,9 @@
     r16 = lax.broadcasted_iota(jnp.int32, (KVL * BATCH * STEPS, PW), 0)
     lanes16 = lax.broadcasted_iota(jnp.int32, (KVL * BATCH * STEPS, PW), 1)
     causal = (r16 // STEPS == lanes16 // R) & (r16 % STEPS <= lanes16 % STEPS)
+
+    def new_here(_):
+        load_new.wait()
 
     def fresh(b):
         stage_new(b)
@@ -338,7 +351,7 @@
         over_g(came, came, zq_s.at[0], zq_r.at[k], g).wait_recv()
         send_own(RES_DEV + k, greeted)
 
-    def attend_slot(cache, row, length, slot, b, j, hold=False):
+    def attend_slot(row, length, slot, b, j, hold=False):
         lane = lax.broadcasted_iota(jnp.int32, (R, 128), 1)
         usable = offset + lax.broadcasted_iota(jnp.int32, (R, pos), 1) < length
         stats = [jnp.zeros((R, 128), F32) for _ in range(KVL)]
@@ -379,20 +392,19 @@
         for i in range(KVL):
             statbuf[pl.ds(pl.multiple_of(i * LW + j * R, R), R), :] = stats[i]
         if not hold:
-            for n in range(1, T):
-                c_o(b, j, n).start()
+            for n, p in greeted:
+                c_o(b, j, n, p).start()
 
     def send_stats(b):
-        for n in range(1, T):
-            c_st(b, n).start()
+        for n, p in greeted:
+            c_st(b, n, p).start()
         rbuf[b, 0] = obuf[b, t]
         rstat[b, 0] = sbuf[b, t]
 
     rest = pl.ds(1, T - 1)
 
     def loaded(_):
-        load_pre.wait()
-        load_res.wait()
+        pltpu.make_async_copy(cache, cache, load_sem.at[4]).wait()
 
     def turn_stats(b):
         turned = statbuf[...].T
@@ -404,7 +416,7 @@
         def _(j):
             s = b * BATCH + j
             whole(s)
-            attend_slot(res, s, kept[0, g * RES_DEV + s], s, b, j, hold)
+            attend_slot(MIG_DEV + s, kept[0, g * RES_DEV + s], s, b, j, hold)
 
         turn_stats(b)
         if not hold:
@@ -416,7 +428,7 @@
             k = (b - STAY) * BATCH + j
             whole(RES_DEV + k)
             held = tab_s[G + k, 0]
-            attend_slot(pre, held % MIG_DEV, held // MIG_DEV, RES_DEV + k, b, j, hold)
+            attend_slot(held % MIG_DEV, held // MIG_DEV, RES_DEV + k, b, j, hold)
 
         turn_stats(b)
         if not hold:
@@ -424,15 +436,15 @@
 
     def send_batch(b):
         for j in range(BATCH):
-            for n in range(1, T):
-                c_o(b, j, n).start()
+            for n, p in greeted:
+                c_o(b, j, n, p).start()
         send_stats(b)
 
     def reach(_):
         if square:
             pl.semaphore_wait(across.at[0], 1)
             for s in (*range(RES_DEV), RES_DEV + mine):
-                send_own(s, greeted[2:])
+                send_own(s, greeted[:1])
 
     def stays():
         pl.loop(0, STAY)(stay_batch)
@@ -445,15 +457,15 @@
         def _(i):
             moved_batch(STAY + turn(i))
 
-    def forward_far(_):
-        @pl.loop(0, far_pairs - 1)
-        def _(i):
-            for j in range(2):
-                forward(2 * turn_in(i) + j)
+    def forward_pair(i):
+        for j in range(2):
+            forward(2 * turn_in(i) + j)
+
+    def forward_rest(_):
+        pl.loop(1, far_pairs - 1)(forward_pair)
 
 
     F, N, L = forward, fresh, late
-    load_new.wait()
     middle = list(range(2, beside))
     early = g < G // 4
 
@@ -463,18 +475,25 @@
             stay_batch(0, False)
             pl.loop(1, STAY)(stay_batch)
 
+    def first_stay_late(_):
+        @pl.when(jnp.logical_not(early))
+        def _():
+            stay_batch(0)
+
     def stays_late(_):
-        pl.when(jnp.logical_not(early))(stays)
+        @pl.when(jnp.logical_not(early))
+        def _():
+            pl.loop(1, STAY)(stay_batch)
 
     def held_late(_):
         pl.when(jnp.logical_not(early))(functools.partial(send_batch, 0))
         for b in range(1, STAY):
             send_batch(b)
 
-    plan = [(L, beside), (N, 0), (L, beside - 2), (L, beside - 1), (reach, 0), (F, beside)]
-    plan += [(N, 1)] + [(L, k) for k in reversed(range(beside - 2))]
-    plan += [(F, beside - 2), (F, beside - 1), (loaded, 0), (stays_early, 0), (N, NB - 1)]
-    plan += [(forward_far, 0)]
+    plan = [(reach, 0), (L, beside), (new_here, 0), (N, 0), (L, beside - 2), (L, beside - 1), (F, beside)]
+    plan += [(N, 1)] + [(L, k + j) for k in reversed(range(0, beside - 2, 2)) for j in range(2)] + [(N, NB - 1)]
+    plan += [(F, beside - 2), (F, beside - 1), (loaded, 0), (stays_early, 0)]
+    plan += [(forward_pair, 0), (first_stay_late, 0), (forward_rest, 0)]
     plan += [(stays_late, 0), (locals_held, 0), (far, 0), (send_batch, NB - 1)]
     plan += [(held_late, 0)]
     plan += [(N, b) for b in range(STAY, NB - 1)]
@@ -485,34 +504,45 @@
         over_t(rstat.at[b, rest], rstat.at[b, rest], st_s.at[0], st_r.at[b], t).wait_recv()
         over_t(rbuf.at[b, rest], rbuf.at[b, rest], o_s.at[0], o_r.at[b], t).wait_recv()
 
-    def merged(b):
+    def factors_of(b):
         tops = [rstat[b, n][0:1] for n in range(T)]
         highest = functools.reduce(jnp.maximum, tops)
-        total = jnp.zeros((1, PW), F32)
-        for n in range(T):
-            factor = jnp.exp(tops[n] - highest)
-            total = total + factor * rstat[b, n][1:2]
-            facbuf[b, n : n + 1, :] = factor
-        columns = facbuf[b].T
-        blended = jnp.zeros((PW, HD), F32)
-        for n in range(T):
-            part = rbuf[b, n].reshape(PW, HD).astype(F32)
-            blended = blended + part * columns[:, n : n + 1]
-        return highest, total, blended
-
-    def finish(b, highest, total, blended):
-        new_top, new_total = nstat[b, 0:1], nstat[b, 1:2]
-        top = jnp.maximum(highest, new_top)
-        old_part, new_part = jnp.exp(highest - top), jnp.exp(new_top - top)
-        inverse = 1.0 / (total * old_part + new_total * new_part)
-        facbuf[NB + b, 0:1, :] = old_part * inverse
-        facbuf[NB + b, 1:2, :] = new_part * inverse
-        columns = facbuf[NB + b].T
-        done = blended * columns[:, 0:1] + nadd[b] * columns[:, 1:2]
+        factors = [jnp.exp(top - highest) for top in tops]
+        total = factors[0] * rstat[b, 0][1:2]
+        for n in range(1, T):
+            total = total + factors[n] * rstat[b, n][1:2]
+        return highest, total, factors
+
+    def columns_of(place, rows):
+        for i, row in enumerate(rows):
+            facbuf[place, i : i + 1, :] = row
+        return facbuf[place].T
+
+    def blend(b, columns):
+        blended = rbuf[b, 0].reshape(PW, HD).astype(F32) * columns[:, 0:1]
+        for n in range(1, T):
+            blended = blended + rbuf[b, n].reshape(PW, HD).astype(F32) * columns[:, n : n + 1]
+        return blended
+
+    def merged(b):
+        highest, total, factors = factors_of(b)
+        return highest, total, blend(b, columns_of(b, factors))
+
+    def with_new(b, highest, total):
+        top = jnp.maximum(highest, nstat[b, 0:1])
+        old_part, new_part = jnp.exp(highest - top), jnp.exp(nstat[b, 0:1] - top)
+        inverse = 1.0 / (total * old_part + nstat[b, 1:2] * new_part)
+        return old_part * inverse, new_part * inverse
+
+    def keep(b, done):
         for j in range(BATCH):
             for i in range(KVL):
                 lo = i * LW + j * R
                 fin[b * BATCH + j, i * R : (i + 1) * R, :] = done[lo : lo + R]
+
+    def finish(b, highest, total, blended):
+        columns = columns_of(NB + b, with_new(b, highest, total))
+        keep(b, blended * columns[:, 0:1] + nadd[b] * columns[:, 1:2])
 
     def put(slot, row):
         for h in range(HB):
@@ -541,9 +571,10 @@
             give_back(STAY + turn(i))
 
     def end_stay(b):
-        finish(b, *merged(b))
-        for j in range(BATCH):
-            put(b * BATCH + j, b * BATCH + j)
+        highest, total, factors = factors_of(b)
+        old, new = with_new(b, highest, total)
+        columns = columns_of(b, [factor * old for factor in factors] + [new])
+        keep(b, blend(b, columns) + nadd[b] * columns[:, T : T + 1])
 
     def returned(b):
         first = (b - STAY) * BATCH
@@ -576,11 +607,14 @@
             end_stay(0)
 
     plan = [(stay_early, 0), (give_far, 0), (give_back, moved[-1]), (stay_late, 0)]
-    plan += [(returned, b) for b in moved] + [(end_moved, b) for b in moved]
-    for b in range(1, STAY):
-        plan += [(arrived, b), (end_stay, b)]
+    last = [moved[0], moved[-1]]
+    plan += [(returned, b) for b in moved[1:-1]] + [(end_moved, b) for b in moved[1:-1]]
+    plan += [(returned, b) for b in last] + [(arrived, b) for b in range(1, STAY)]
+    plan += [(end_moved, b) for b in last] + [(end_stay, b) for b in range(1, STAY)]
     for step, p in plan:
         step(p)
+    for j in range(RES_DEV):
+        put(j, j)
     for l in range(MIG_DEV):
         k_of = 0
         for k in range(G):
@@ -626,16 +660,13 @@
         in_specs=[hbm] * 8,
         out_specs=vmem,
         scratch_shapes=[
-            pltpu.VMEM((1, kept_tokens.shape[0]), jnp.int32),
-            pltpu.VMEM((1, prefill_slot.shape[0]), jnp.int32),
-            pltpu.VMEM((1, decode_slot.shape[0]), jnp.int32),
+            pltpu.VMEM((3, kept_tokens.shape[0]), jnp.int32),
             pltpu.SMEM((1, resident_kept.shape[0]), jnp.int32),
             pltpu.VMEM((2 * G, 128), jnp.int32),
             pltpu.SMEM((2 * G, 128), jnp.int32),
             pltpu.VMEM(queries.shape, BF16),
             pltpu.VMEM(new_entries.shape, BF16),
-            pltpu.VMEM(resident_cache.shape, BF16),
-            pltpu.VMEM(prefill_cache.shape, BF16),
+            pltpu.VMEM((PER_GROUP, *resident_cache.shape[1:]), BF16),
             pltpu.VMEM((T, RES_DEV + G, RB, HD), BF16),
             pltpu.VMEM((G, RB, HD), BF16),
             pltpu.VMEM((PER_GROUP, RB, HD), F32),
@@ -644,7 +675,7 @@
             pltpu.VMEM((NB, T, 2, PW), F32),
             pltpu.VMEM((NB, T, 2, PW), F32),
             pltpu.VMEM((PW, 128), F32),
-            pltpu.VMEM((2 * NB, max(8, T), PW), F32),
+            pltpu.VMEM((2 * NB, -(-(T + 1) // 8) * 8, PW), F32),
             pltpu.VMEM((G, KVL, R, HD), BF16),
             pltpu.VMEM((G, KVL, R, HD), BF16),
             pltpu.VMEM((NB - STAY, 2, PW), F32),
@@ -654,8 +685,7 @@
             pltpu.VMEM((NB, PW, HD), F32),
             pltpu.VMEM((NB * BATCH, RB, HD), F32),
             dma((5,)),
-            dma((4,)),
-            pltpu.SemaphoreType.REGULAR((G,)),
+            pltpu.SemaphoreType.REGULAR((G // 2 if G & (G - 1) == 0 else G,)),
             pltpu.SemaphoreType.REGULAR((1,)),
             dma((1,)),
             dma((G,)),

time: 25.4 us -> 24.9 us (0.980)
  Pallas kernels: 24.5 us -> 23.8 us
    pallas_call x1, Pallas kernels: 24.5 us -> 23.8 us  [body(): pl.pallas_call(functools.partial(kernel, G, T), out_shape=pltpu.VMEM(quer...]
where the time goes in v3:
time: 24.9 us; the launch traced here: 24.5 us
  Pallas kernels  23.8 us (96%)
  local copies, waits for them, and re-layouts  0.68 us (3%)
    pallas_call x1, Pallas kernels, body(): pl.pallas_call(functools.partial(kernel, G, T), out_shape=pltpu.VMEM(quer...  23.8 us
    unnamed x1, local copies, waits for them, and re-layouts  0.68 us

profile of v3, /device:TPU:0, one launch (start us, length us, event | category | flops | bytes accessed | tf_op | source)
XLA Modules:
  0.0 24.5 jit_solution(7831197916246677092)
XLA Ops:
  0.0 23.8 %shard_map.82 = bf16[12,4,2048]{2,1,0:T(4,128)(2,1)S(1)} custom-call(s32[1,64]{1,0:T(1,128)} %bitcast.4, s32[1,64]{1,0:T(1,128)} %bitcast.5, s32[1,64]{1,0:T(1,128)} %bitcast.6, s32[1,32]{1,0:T(1,128)} %bitcast.7, bf16[12,4,2048]{2,1,0:T(4,128)(2,1)} %q_hbm.1, bf16[12,4,2048]{2,1,0:T(4,128)(2,1)} %new_hbm.1, bf16[4,128,2048]{2,1,0:T(8,128)(2,1)} %res_hbm.1, ...), custom_call_target="tpu_custom_call" | custom-call | tf_op jit(solution)/shard_map/pallas_call | solution.py:657
  23.8 0.7 %copy.10 = bf16[12,4,2048]{2,1,0:T(4,128)(2,1)} copy(bf16[12,4,2048]{2,1,0:T(4,128)(2,1)S(1)} %shard_map.82) | data formatting | bytes 393216

commit v4 on v3

--- a/solution.py
+++ b/solution.py
@@ -490,7 +490,7 @@
         for b in range(1, STAY):
             send_batch(b)
 
-    plan = [(reach, 0), (L, beside), (new_here, 0), (N, 0), (L, beside - 2), (L, beside - 1), (F, beside)]
+    plan = [(new_here, 0), (N, 0), (reach, 0), (L, beside), (L, beside - 2), (L, beside - 1), (F, beside)]
     plan += [(N, 1)] + [(L, k + j) for k in reversed(range(0, beside - 2, 2)) for j in range(2)] + [(N, NB - 1)]
     plan += [(F, beside - 2), (F, beside - 1), (loaded, 0), (stays_early, 0)]
     plan += [(forward_pair, 0), (first_stay_late, 0), (forward_rest, 0)]
@@ -607,10 +607,22 @@
             end_stay(0)
 
     plan = [(stay_early, 0), (give_far, 0), (give_back, moved[-1]), (stay_late, 0)]
-    last = [moved[0], moved[-1]]
+    waits_long = early & (lax.rem(g, 2) == 1)
+
+    def end_beside(_):
+        returned(moved[-1])
+        end_moved(moved[-1])
+
+    def beside_soon(_):
+        pl.when(jnp.logical_not(waits_long))(functools.partial(end_beside, 0))
+
+    def beside_last(_):
+        pl.when(waits_long)(functools.partial(end_beside, 0))
+
     plan += [(returned, b) for b in moved[1:-1]] + [(end_moved, b) for b in moved[1:-1]]
-    plan += [(returned, b) for b in last] + [(arrived, b) for b in range(1, STAY)]
-    plan += [(end_moved, b) for b in last] + [(end_stay, b) for b in range(1, STAY)]
+    plan += [(beside_soon, 0), (returned, moved[0])] + [(arrived, b) for b in range(1, STAY)]
+    plan += [(end_moved, moved[0])] + [(end_stay, b) for b in range(1, STAY)]
+    plan += [(beside_last, 0)]
     for step, p in plan:
         step(p)
     for j in range(RES_DEV):

time: 24.9 us -> 24.8 us (level)
  no operation moved by 1% of the time
where the time goes in v4:
time: 24.8 us; the launch traced here: 24.5 us
  Pallas kernels  23.8 us (96%)
  local copies, waits for them, and re-layouts  0.68 us (3%)
    pallas_call x1, Pallas kernels, body(): pl.pallas_call(functools.partial(kernel, G, T), out_shape=pltpu.VMEM(quer...  23.8 us
    unnamed x1, local copies, waits for them, and re-layouts  0.68 us

profile of v4, /device:TPU:0, one launch (start us, length us, event | category | flops | bytes accessed | tf_op | source)
XLA Modules:
  0.0 24.5 jit_solution(11871803797007276443)
XLA Ops:
  0.0 23.8 %shard_map.82 = bf16[12,4,2048]{2,1,0:T(4,128)(2,1)S(1)} custom-call(s32[1,64]{1,0:T(1,128)} %bitcast.4, s32[1,64]{1,0:T(1,128)} %bitcast.5, s32[1,64]{1,0:T(1,128)} %bitcast.6, s32[1,32]{1,0:T(1,128)} %bitcast.7, bf16[12,4,2048]{2,1,0:T(4,128)(2,1)} %q_hbm.1, bf16[12,4,2048]{2,1,0:T(4,128)(2,1)} %new_hbm.1, bf16[4,128,2048]{2,1,0:T(8,128)(2,1)} %res_hbm.1, ...), custom_call_target="tpu_custom_call" | custom-call | tf_op jit(solution)/shard_map/pallas_call | solution.py:669
  23.8 0.7 %copy.10 = bf16[12,4,2048]{2,1,0:T(4,128)(2,1)} copy(bf16[12,4,2048]{2,1,0:T(4,128)(2,1)S(1)} %shard_map.82) | data formatting | bytes 393216

commit v5 on v4

--- a/solution.py
+++ b/solution.py
@@ -191,12 +191,20 @@
 
     def send_own(s, devs):
         own = qall.at[t, s]
+        sem = place(s) if isinstance(s, int) else STAY + s - RES_DEV
         for _, dev in devs:
-            over_t(own, own, q_s.at[0], q_r.at[s], dev).start()
-
-    def whole(s):
-        rest = qall.at[pl.ds(0, T - 1), s]
-        over_t(rest, rest, q_s.at[0], q_r.at[s], t).wait_recv()
+            over_t(own, own, q_s.at[0], q_r.at[sem], dev).start()
+
+    def place(s):
+        return s // BATCH if s < RES_DEV else STAY + s - RES_DEV
+
+    def whole(k):
+        rest = qall.at[pl.ds(0, T - 1), RES_DEV + k]
+        over_t(rest, rest, q_s.at[0], q_r.at[STAY + k], t).wait_recv()
+
+    def whole_stays(b):
+        rest = qall.at[pl.ds(0, T - 1), pl.ds(b * BATCH, BATCH)]
+        over_t(rest, rest, q_s.at[0], q_r.at[b], t).wait_recv()
 
     def c_o(b, j, n, p):
         rows = pl.ds(pl.multiple_of(j * R, R), R)
@@ -256,8 +264,8 @@
         pl.semaphore_signal(barrier, inc=1, device_id=(g, dev), device_id_type=MESH)
     load_q = pltpu.make_async_copy(q_hbm, q_in, load_sem.at[2])
     load_new = pltpu.make_async_copy(new_hbm, new_in, load_sem.at[3])
-    load_pre = pltpu.make_async_copy(pre_hbm, cache.at[0:MIG_DEV], load_sem.at[4])
-    load_res = pltpu.make_async_copy(res_hbm, cache.at[MIG_DEV:PER_GROUP], load_sem.at[4])
+    load_pre = pltpu.make_async_copy(pre_hbm, cache.at[0:MIG_DEV], load_sem.at[1])
+    load_res = pltpu.make_async_copy(res_hbm, cache.at[MIG_DEV:PER_GROUP], load_sem.at[1])
     tables = [
         pltpu.make_async_copy(src, dst, load_sem.at[i // 3])
         for i, (src, dst) in enumerate(
@@ -404,7 +412,7 @@
     rest = pl.ds(1, T - 1)
 
     def loaded(_):
-        pltpu.make_async_copy(cache, cache, load_sem.at[4]).wait()
+        pltpu.make_async_copy(cache, cache, load_sem.at[1]).wait()
 
     def turn_stats(b):
         turned = statbuf[...].T
@@ -412,10 +420,11 @@
             sbuf[b, tt] = turned[2 * tt : 2 * tt + 2, :]
 
     def stay_batch(b, hold=True):
+        whole_stays(b)
+
         @pl.loop(0, BATCH)
         def _(j):
             s = b * BATCH + j
-            whole(s)
             attend_slot(MIG_DEV + s, kept[0, g * RES_DEV + s], s, b, j, hold)
 
         turn_stats(b)
@@ -426,7 +435,7 @@
         @pl.loop(0, BATCH)
         def _(j):
             k = (b - STAY) * BATCH + j
-            whole(RES_DEV + k)
+            whole(k)
             held = tab_s[G + k, 0]
             attend_slot(held % MIG_DEV, held // MIG_DEV, RES_DEV + k, b, j, hold)
 
@@ -593,6 +602,13 @@
         )
         finish(b, stats[0:1], stats[1:2], blended)
 
+    slots = []
+    for l in range(MIG_DEV):
+        k_of = 0
+        for k in range(G):
+            k_of = jnp.where(tab_s[k, 0] == RES_DEV + l, k, k_of)
+        slots.append(k_of)
+
     moved = list(range(STAY, NB))
     def stay_early(_):
         @pl.when(early)
@@ -628,10 +644,7 @@
     for j in range(RES_DEV):
         put(j, j)
     for l in range(MIG_DEV):
-        k_of = 0
-        for k in range(G):
-            k_of = jnp.where(tab_s[k, 0] == RES_DEV + l, k, k_of)
-        put(RES_DEV + k_of, RES_DEV + l)
+        put(RES_DEV + slots[l], RES_DEV + l)
 
     others = pl.ds(1, G - 1)
     over_g(zq.at[others], zq.at[others], zq_s.at[0], zq_r.at[0], g).wait_send()
@@ -696,13 +709,13 @@
             pltpu.VMEM((NB, 2, PW), F32),
             pltpu.VMEM((NB, PW, HD), F32),
             pltpu.VMEM((NB * BATCH, RB, HD), F32),
-            dma((5,)),
+            dma((4,)),
             pltpu.SemaphoreType.REGULAR((G // 2 if G & (G - 1) == 0 else G,)),
             pltpu.SemaphoreType.REGULAR((1,)),
             dma((1,)),
-            dma((G,)),
+            dma((G - 1,)),
             dma((1,)),
-            dma((RES_DEV + G,)),
+            dma((STAY + G,)),
             dma((1,)),
             dma((NB,)),
             dma((1,)),

time: 24.8 us -> 24.7 us (level)
  no operation moved by 1% of the time
where the time goes in v5:
time: 24.7 us; the launch traced here: 24.5 us
  Pallas kernels  23.8 us (96%)
  local copies, waits for them, and re-layouts  0.68 us (3%)
    pallas_call x1, Pallas kernels, body(): pl.pallas_call(functools.partial(kernel, G, T), out_shape=pltpu.VMEM(quer...  23.8 us
    unnamed x1, local copies, waits for them, and re-layouts  0.68 us

profile of v5, /device:TPU:0, one launch (start us, length us, event | category | flops | bytes accessed | tf_op | source)
XLA Modules:
  0.0 24.5 jit_solution(3430837638886086956)
XLA Ops:
  0.0 23.8 %shard_map.82 = bf16[12,4,2048]{2,1,0:T(4,128)(2,1)S(1)} custom-call(s32[1,64]{1,0:T(1,128)} %bitcast.4, s32[1,64]{1,0:T(1,128)} %bitcast.5, s32[1,64]{1,0:T(1,128)} %bitcast.6, s32[1,32]{1,0:T(1,128)} %bitcast.7, bf16[12,4,2048]{2,1,0:T(4,128)(2,1)} %q_hbm.1, bf16[12,4,2048]{2,1,0:T(4,128)(2,1)} %new_hbm.1, bf16[4,128,2048]{2,1,0:T(8,128)(2,1)} %res_hbm.1, ...), custom_call_target="tpu_custom_call" | custom-call | tf_op jit(solution)/shard_map/pallas_call | solution.py:682
  23.8 0.7 %copy.10 = bf16[12,4,2048]{2,1,0:T(4,128)(2,1)} copy(bf16[12,4,2048]{2,1,0:T(4,128)(2,1)S(1)} %shard_map.82) | data formatting | bytes 393216

commit v6 on v4

--- a/solution.py
+++ b/solution.py
@@ -361,14 +361,18 @@
         all_scores = []
         for tt, i in units:
             kv = (tt * KVL + i) * KVH // (T * KVL)
-            asked = qall[tt, slot, i * R : (i + W) * R, :]
-            keys = jnp.concatenate(
-                [cache[row, :, (kv + w) * HD : (kv + w + 1) * HD] for w in range(W)], axis=0
+            parts = [qall[tt, slot, (i + w) * R : (i + w + 1) * R, :] for w in range(W)]
+            blank = jnp.zeros((R, HD), BF16)
+            asked = jnp.concatenate(
+                [
+                    jnp.concatenate([parts[w] if v == w else blank for v in range(W)], axis=1)
+                    for w in range(W)
+                ],
+                axis=0,
             )
+            keys = cache[row, :, kv * HD : (kv + W) * HD]
             scores = lax.dot_general(asked, keys, NT, preferred_element_type=F32)
-            all_scores.append(
-                [scores[w * R : (w + 1) * R, w * pos : (w + 1) * pos] * SCALE for w in range(W)]
-            )
+            all_scores.append([scores[w * R : (w + 1) * R] * SCALE for w in range(W)])
         all_weights = []
         for (tt, i), scores in zip(units, all_scores):
             rounded = []

time: 24.8 us -> 24.8 us (level)
  no operation moved by 1% of the time
where the time goes in v6:
time: 24.8 us; the launch traced here: 24.5 us
  Pallas kernels  23.8 us (96%)
  local copies, waits for them, and re-layouts  0.68 us (3%)
    pallas_call x1, Pallas kernels, body(): pl.pallas_call(functools.partial(kernel, G, T), out_shape=pltpu.VMEM(quer...  23.8 us
    unnamed x1, local copies, waits for them, and re-layouts  0.68 us

profile of v6, /device:TPU:0, one launch (start us, length us, event | category | flops | bytes accessed | tf_op | source)
XLA Modules:
  0.0 24.5 jit_solution(18228951632136694470)
XLA Ops:
  0.0 23.8 %shard_map.82 = bf16[12,4,2048]{2,1,0:T(4,128)(2,1)S(1)} custom-call(s32[1,64]{1,0:T(1,128)} %bitcast.4, s32[1,64]{1,0:T(1,128)} %bitcast.5, s32[1,64]{1,0:T(1,128)} %bitcast.6, s32[1,32]{1,0:T(1,128)} %bitcast.7, bf16[12,4,2048]{2,1,0:T(4,128)(2,1)} %q_hbm.1, bf16[12,4,2048]{2,1,0:T(4,128)(2,1)} %new_hbm.1, bf16[4,128,2048]{2,1,0:T(8,128)(2,1)} %res_hbm.1, ...), custom_call_target="tpu_custom_call" | custom-call | tf_op jit(solution)/shard_map/pallas_call | solution.py:673
  23.8 0.7 %copy.10 = bf16[12,4,2048]{2,1,0:T(4,128)(2,1)} copy(bf16[12,4,2048]{2,1,0:T(4,128)(2,1)S(1)} %shard_map.82) | data formatting | bytes 393216
